TPU v7x, 256 devices: a whole 4x4x8 slice. The times are simulated.
256 devices in a mesh: cache: 64 (over y, z, core), group: 4 (over x).
Axes of the slice: x: 4, y: 4, z: 8, core: 2. Of those that a mesh axis runs over, the one named last changes fastest.
Arguments:
- queries: bfloat16 [256, 4096], P('cache'), may hold values from -240 to 240
- request_of: int32 [256], P('cache'), may hold values from 0 to 15, as said below
- selected: int32 [256, 8, 4], P('cache', 'group'), may hold values from 0 to 127, as said below
- cache_keys: bfloat16 [16, 8, 16384, 128], P(None, 'group', 'cache'), may hold values from -6 to 6
- cache_values: bfloat16 [16, 8, 16384, 128], P(None, 'group', 'cache'), may hold values from -6 to 6
- recent_keys: bfloat16 [256, 8, 1024, 128], P('cache', None, 'group'), may hold values from -6 to 6
- recent_values: bfloat16 [256, 8, 1024, 128], P('cache', None, 'group'), may hold values from -6 to 6
Outputs:
- attended: bfloat16 [256, 4096], P('cache', 'group')
Inputs may be any that keep to these rules, and one draw needn't show every extreme that they name: `request_of`: each prompt is read by exactly 16 slots. `selected`: for each slot and key-value head the 4 block ids have distinct owners id // 2; the 4 slots of one index of cache, with the key-value heads of one index of group, select at most 1 block held by any one owner, and exactly 1 from some owner.
All inputs are finite; a program needn't handle non-finite values.
Results may differ from a plain program's by a relative error of at most 0.0015.
Values may be sent and summed in bfloat16 or wider, within the bound.
A program may use at most 64 MiB of HBM per device.

v0:
```python
import math

import jax
import jax.numpy as jnp
from jax import lax
from jax.sharding import PartitionSpec as P

BLOCK = 128


def sent_to_all(array, axis):
    copies = jnp.broadcast_to(array, (lax.axis_size(axis), *array.shape))
    return lax.all_to_all(copies, axis, split_axis=0, concat_axis=0, tiled=True)


def in_order(blocks, dim):
    lengths = list(blocks.shape[1:])
    lengths[dim] *= blocks.shape[0]
    return jnp.moveaxis(blocks, 0, dim).reshape(lengths)


def collect(array, axis, dim):
    blocks = sent_to_all(array, axis)
    return in_order(blocks, dim)


def in_one_piece(arrays, axis, dim, along):
    columns = [a.reshape(*a.shape[:along], -1) for a in arrays]
    both = jnp.concatenate(columns, axis=along)
    out, at, outs = (collect(both, axis, dim), 0, [])
    for a, column in zip(arrays, columns):
        share = out[..., at : at + column.shape[along]]
        outs.append(share.reshape(*share.shape[:along], *a.shape[along:]))
        at += column.shape[along]
    return tuple(outs)


def sent_together(arrays, axis, split_dim, concat_dim, along):
    widths = [math.prod(a.shape[along:]) for a in arrays]
    both = jnp.concatenate(
        [a.reshape(*a.shape[:along], w) for a, w in zip(arrays, widths)], axis=along
    )
    out = lax.all_to_all(both, axis, split_axis=split_dim, concat_axis=concat_dim, tiled=True)
    blocks = jnp.split(out, [sum(widths[:k]) for k in range(1, len(widths))], axis=along)
    return tuple((b.reshape(*out.shape[:along], *a.shape[along:]) for a, b in zip(arrays, blocks)))


def partial_attention(query_heads, key_rows, value_rows, score_scale):
    scores = (
        jnp.einsum("rhgd,rhnd->rhgn", query_heads, key_rows, preferred_element_type=jnp.float32)
        * score_scale
    )
    highest = jnp.max(scores, axis=-1)
    exponent = jnp.exp(scores - highest[..., None])
    totals = jnp.sum(exponent, axis=-1)
    summed = jnp.einsum(
        "rhgn,rhnd->rhgd", exponent, value_rows.astype(jnp.float32), precision=lax.Precision.HIGHEST
    )
    return (summed, highest, totals)


def combine(summed, highest, totals):
    peak_value = jnp.max(highest, axis=0)
    factor = jnp.exp(highest - peak_value[None])
    weight = jnp.sum(factor * totals, axis=0)
    return jnp.sum(factor[..., None] * summed, axis=0) / weight[..., None]


def owner_plan(
    all_prompts,
    all_selected,
    cache_keys,
    cache_values,
    owner_count,
    row_count,
    mine_heads,
    top_count,
    head_dim,
):
    per_owner = cache_keys.shape[2] // BLOCK
    wanted = row_count * mine_heads * top_count
    capacity = (wanted + owner_count - 1) // owner_count
    entry = jnp.arange(wanted, dtype=jnp.int32)
    dest_selected = all_selected.reshape(owner_count, wanted)
    held_here = dest_selected // per_owner == lax.axis_index("cache")
    rank_here = jnp.cumsum(held_here.astype(jnp.int32), axis=1) - 1
    place = jnp.arange(capacity, dtype=jnp.int32)
    picks = held_here[:, None, :] & (rank_here[:, None, :] == place[None, :, None])
    slot_entry = jnp.sum(jnp.where(picks, entry[None, None, :], 0), axis=2)
    slot_block = jnp.sum(jnp.where(picks, dest_selected[:, None, :], 0), axis=2) % per_owner
    slot_row = slot_entry // (mine_heads * top_count)
    slot_head = slot_entry // top_count % mine_heads
    slot_prompt = jnp.take_along_axis(all_prompts.reshape(owner_count, row_count), slot_row, axis=1)
    key_blocks = cache_keys.reshape(cache_keys.shape[0], mine_heads, per_owner, BLOCK, head_dim)[
        slot_prompt, slot_head, slot_block
    ]
    value_blocks = cache_values.reshape(
        cache_values.shape[0], mine_heads, per_owner, BLOCK, head_dim
    )[slot_prompt, slot_head, slot_block]
    return (slot_row, slot_head, key_blocks, value_blocks)


def per_device(queries, request_of, selected, cache_keys, cache_values, recent_keys, recent_values):
    row_count = queries.shape[0]
    heads_kv = recent_keys.shape[1]
    head_dim = recent_keys.shape[3]
    per_kv = queries.shape[1] // (heads_kv * head_dim)
    mine_heads = selected.shape[1]
    top_count = selected.shape[2]
    score_scale = head_dim ** (-0.5)
    all_heads = queries.reshape(row_count, heads_kv, per_kv, head_dim)
    own_heads = lax.dynamic_slice_in_dim(
        all_heads, lax.axis_index("group") * mine_heads, mine_heads, 1
    )
    owner_count = lax.axis_size("cache")
    per_owner = cache_keys.shape[2] // BLOCK
    wanted = row_count * mine_heads * top_count
    entry = jnp.arange(wanted, dtype=jnp.int32)
    own_flat = selected.reshape(wanted)
    source = own_flat // per_owner
    earlier = (source[:, None] == source[None, :]) & (entry[None, :] < entry[:, None])
    source_rank = jnp.sum(earlier.astype(jnp.int32), axis=1)
    all_prompts, all_selected, gathered = (
        *in_one_piece((request_of, selected), "cache", 0, 1),
        collect(own_heads.reshape(row_count, mine_heads * per_kv * head_dim), "cache", 0),
    )
    slot_row, slot_head, key_blocks, value_blocks = owner_plan(
        all_prompts,
        all_selected,
        cache_keys,
        cache_values,
        owner_count,
        row_count,
        mine_heads,
        top_count,
        head_dim,
    )
    gathered = gathered.reshape(owner_count, row_count, mine_heads, per_kv, head_dim)
    owner_index = jnp.arange(owner_count, dtype=jnp.int32)[:, None]
    slot_queries = gathered[owner_index, slot_row, slot_head]
    summed, highest, totals = partial_attention(slot_queries, key_blocks, value_blocks, score_scale)
    summed, highest, totals = (
        lax.all_to_all(summed, "cache", split_axis=0, concat_axis=0, tiled=True),
        lax.all_to_all(highest, "cache", split_axis=0, concat_axis=0, tiled=True),
        lax.all_to_all(totals, "cache", split_axis=0, concat_axis=0, tiled=True),
    )
    far_summed = jnp.moveaxis(
        summed[source, source_rank].reshape(row_count, mine_heads, top_count, per_kv, head_dim),
        2,
        0,
    )
    far_highest = jnp.moveaxis(
        highest[source, source_rank].reshape(row_count, mine_heads, top_count, per_kv), 2, 0
    )
    far_totals = jnp.moveaxis(
        totals[source, source_rank].reshape(row_count, mine_heads, top_count, per_kv), 2, 0
    )
    summed, highest, totals = partial_attention(all_heads, recent_keys, recent_values, score_scale)
    near_summed, near_highest, near_totals = sent_together(
        (summed[None], highest[None], totals[None]), "group", 2, 0, 4
    )
    merged = combine(
        jnp.concatenate([far_summed, near_summed], axis=0),
        jnp.concatenate([far_highest, near_highest], axis=0),
        jnp.concatenate([far_totals, near_totals], axis=0),
    )
    return merged.reshape(row_count, mine_heads * per_kv * head_dim).astype(jnp.bfloat16)


def solution(mesh):
    return jax.shard_map(
        per_device,
        mesh=mesh,
        in_specs=(
            P("cache", None),
            P("cache"),
            P("cache", "group", None),
            P(None, "group", "cache", None),
            P(None, "group", "cache", None),
            P("cache", None, "group", None),
            P("cache", None, "group", None),
        ),
        out_specs=P("cache", "group"),
        check_vma=False,
    )
```

profile of v0, /device:TPU:1, one launch (start us, length us, event | category | flops | bytes accessed | tf_op | source)
XLA Modules:
  0.0 113.9 jit_solution(30961070402199036)
XLA Ops:
  0.0 0.9 copy.127
  0.9 0.8 reshape.661
  1.7 0.7 broadcast_in_dim.23
  2.4 13.1 %all-to-all-start.1 = ((s32[64,4,9]{2,1,0:T(4,128)}), s32[64,4,9]{2,1,0:T(4,128)S(1)}, u32[]{:S(2)}, u32[]{:S(2)}) async-start(s32[64,4,9]{2,1,0:T(4,128)} %broadcast_in_dim.23), calls=%async_computation.1 | async-start | bytes 262144 | tf_op jit(solution)/shard_map/all_to_all | solution.py:13
  15.6 0.8 reshape.667
  16.3 0.8 reshape.666
  17.1 0.8 reshape.658
  17.9 0.2 convert_reduce_fusion
  18.1 2.4 %fusion.27 = (f32[4,8,4]{2,1,0:T(8,128)S(1)}, f32[4,8,4,256]{3,2,1,0:T(4,128)S(1)}) fusion(bf16[4,8,4,128]{3,2,1,0:T(4,128)(2,1)S(1)} %reshape.658, bf16[4,8,256,128]{3,2,1,0:T(8,128)(2,1)} %param.12), kind=kOutput, calls=%fused_computation.101 | convolution fusion | flops 8454016 | bytes 2261504 | tf_op jit(solution)/shard_map/rhgd,rhnd->rhgn/dot_general | solution.py:50
  20.5 0.2 fusion.1
  20.8 1.0 convolution_bitcast_fusion.1
  21.8 0.3 copy.132
  22.1 0.3 copy.131
  22.6 0.6 copy.133
  23.2 2.7 %all-to-all-done.1 = s32[64,4,9]{2,1,0:T(4,128)S(1)} async-done(((s32[64,4,9]{2,1,0:T(4,128)}), s32[64,4,9]{2,1,0:T(4,128)S(1)}, u32[]{:S(2)}, u32[]{:S(2)}) %all-to-all-start.1) | async-done | bytes 9248 | tf_op jit(solution)/shard_map/all_to_all | solution.py:13
  25.9 4.0 %all-to-all-start.3 = ((f32[1,4,8,4,130]{4,3,1,0,2:T(4,128)}), f32[1,4,8,4,130]{4,3,1,0,2:T(4,128)S(1)}, u32[]{:S(2)}, u32[]{:S(2)}) async-start(f32[1,4,8,4,130]{4,3,1,0,2:T(4,128)} %copy.133), calls=%async_computation.3 | async-start | bytes 262144 | tf_op jit(solution)/shard_map/all_to_all | solution.py:43
  30.2 0.2 reduce_window_sum.11
  30.4 0.1 select_reduce_fusion.1
  30.6 4.1 %all-to-all-done.3 = f32[1,4,8,4,130]{4,3,1,0,2:T(4,128)S(1)} async-done(((f32[1,4,8,4,130]{4,3,1,0,2:T(4,128)}), f32[1,4,8,4,130]{4,3,1,0,2:T(4,128)S(1)}, u32[]{:S(2)}, u32[]{:S(2)}) %all-to-all-start.3) | async-done | bytes 66592 | tf_op jit(solution)/shard_map/all_to_all | solution.py:43
  34.7 0.9 broadcast_in_dim.22
  35.7 9.1 %all-to-all-start = ((bf16[64,4,1024]{2,1,0:T(4,128)(2,1)}), bf16[64,4,1024]{2,1,0:T(4,128)(2,1)S(1)}, u32[]{:S(2)}, u32[]{:S(2)}) async-start(bf16[64,4,1024]{2,1,0:T(4,128)(2,1)} %broadcast_in_dim.22), calls=%async_computation | async-start | bytes 1048576 | tf_op jit(solution)/shard_map/all_to_all | solution.py:13
  44.9 0.1 reshape_reshape.14
  45.0 0.8 gather_fusion.6
  45.9 2.2 %gather_fusion.1 = bf16[64,128,128]{2,1,0:T(8,128)(2,1)} fusion(bf16[16,2,2,128,128]{4,3,2,1,0:T(8,128)(2,1)S(1)} %bitcast.86, s32[64]{0:T(128)S(1)} %or_bitcast_fusion.1), kind=kCustom, calls=%fused_computation.1 | custom fusion | bytes 4195072 | tf_op jit(solution)/shard_map/gather | solution.py:94
  48.0 3.8 %gather_fusion.3 = bf16[64,128,128]{2,1,0:T(8,128)(2,1)} fusion(bf16[16,2,2,128,128]{4,3,2,1,0:T(8,128)(2,1)} %bitcast.87, s32[64]{0:T(128)S(1)} %or_bitcast_fusion.1), kind=kCustom, calls=%fused_computation.3 | custom fusion | bytes 4195072 | tf_op jit(solution)/shard_map/gather | solution.py:97
  52.0 0.2 fusion.26
  52.3 0.3 copy.153
  52.6 0.3 copy.155
  52.9 9.2 %all-to-all-done = bf16[64,4,1024]{2,1,0:T(4,128)(2,1)S(1)} async-done(((bf16[64,4,1024]{2,1,0:T(4,128)(2,1)}), bf16[64,4,1024]{2,1,0:T(4,128)(2,1)S(1)}, u32[]{:S(2)}, u32[]{:S(2)}) %all-to-all-start) | async-done | bytes 524320 | tf_op jit(solution)/shard_map/all_to_all | solution.py:13
  62.0 0.2 reshape_reshape.11
  62.2 0.8 gather_fusion
  63.1 3.5 %fusion.28 = (f32[64,4]{1,0:T(8,128)}, f32[64,4,128]{2,1,0:T(4,128)S(1)}) fusion(bf16[64,4,128]{2,1,0:T(4,128)(2,1)S(1)} %gather_fusion, bf16[64,128,128]{2,1,0:T(8,128)(2,1)} %gather_fusion.1), kind=kOutput, calls=%fused_computation.102 | convolution fusion | flops 8453888 | bytes 2294784 | tf_op jit(solution)/shard_map/rhgd,rhnd->rhgn/dot_general | solution.py:50
  66.5 6.3 %all-to-all-start.2 = ((f32[64,1,4]{2,1,0:T(1,128)}), f32[64,1,4]{2,1,0:T(1,128)S(1)}, u32[]{:S(2)}, u32[]{:S(2)}) async-start(f32[64,1,4]{2,1,0:T(1,128)} %bitcast.13), calls=%async_computation.2 | async-start | bytes 65536 | tf_op jit(solution)/shard_map/all_to_all | solution.py:144
  72.8 1.6 %fusion.2 = f32[64,4]{1,0:T(8,128)} fusion(f32[64,4,128]{2,1,0:T(4,128)S(1)} %get-tuple-element.19, f32[64,4]{1,0:T(8,128)} %get-tuple-element.18), kind=kLoop, calls=%fused_computation.19 | loop fusion | flops 65280 | bytes 133120 | tf_op jit(solution)/shard_map/reduce_sum | solution.py:55
  74.4 7.7 %all-to-all-done.2 = f32[64,1,4]{2,1,0:T(1,128)S(1)} async-done(((f32[64,1,4]{2,1,0:T(1,128)}), f32[64,1,4]{2,1,0:T(1,128)S(1)}, u32[]{:S(2)}, u32[]{:S(2)}) %all-to-all-start.2) | async-done | bytes 1056 | tf_op jit(solution)/shard_map/all_to_all | solution.py:144
  82.1 4.7 %all-to-all-start.5 = ((f32[64,1,4]{2,1,0:T(1,128)}), f32[64,1,4]{2,1,0:T(1,128)S(1)}, u32[]{:S(2)}, u32[]{:S(2)}) async-start(f32[64,1,4]{2,1,0:T(1,128)} %bitcast.32), calls=%async_computation.5 | async-start | bytes 65536 | tf_op jit(solution)/shard_map/all_to_all | solution.py:145
  86.8 4.1 %convolution_bitcast_fusion = f32[64,1,4,128]{3,2,1,0:T(4,128)} fusion(bf16[64,128,128]{2,1,0:T(8,128)(2,1)} %gather_fusion.3, f32[64,4,128]{2,1,0:T(4,128)S(1)} %get-tuple-element.19, f32[64,4]{1,0:T(8,128)} %get-tuple-element.18), kind=kOutput, calls=%fused_computation.7 | convolution fusion | flops 50364416 | bytes 2360320 | tf_op jit(solution)/shard_map/rhgn,rhnd->rhgd/dot_general | solution.py:56
  90.9 0.6 gather_fusion.2
  91.5 0.1 copy.148
  91.6 4.6 %all-to-all-done.5 = f32[64,1,4]{2,1,0:T(1,128)S(1)} async-done(((f32[64,1,4]{2,1,0:T(1,128)}), f32[64,1,4]{2,1,0:T(1,128)S(1)}, u32[]{:S(2)}, u32[]{:S(2)}) %all-to-all-start.5) | async-done | bytes 1056 | tf_op jit(solution)/shard_map/all_to_all | solution.py:145
  96.3 5.8 %all-to-all-start.4 = ((f32[64,1,4,128]{3,2,1,0:T(4,128)}), f32[64,1,4,128]{3,2,1,0:T(4,128)S(1)}, u32[]{:S(2)}, u32[]{:S(2)}) async-start(f32[64,1,4,128]{3,2,1,0:T(4,128)} %convolution_bitcast_fusion), calls=%async_computation.4 | async-start | bytes 262144 | tf_op jit(solution)/shard_map/all_to_all | solution.py:143
  102.2 0.6 gather_fusion.5
  102.8 0.1 copy.154
  102.9 0.2 fusion.15
  103.3 9.2 %all-to-all-done.4 = f32[64,1,4,128]{3,2,1,0:T(4,128)S(1)} async-done(((f32[64,1,4,128]{3,2,1,0:T(4,128)}), f32[64,1,4,128]{3,2,1,0:T(4,128)S(1)}, u32[]{:S(2)}, u32[]{:S(2)}) %all-to-all-start.4) | async-done | bytes 131104 | tf_op jit(solution)/shard_map/all_to_all | solution.py:143
  112.4 0.6 gather_fusion.4
  113.1 0.1 fusion
  113.3 0.6 convert_element_type.17
  (33 shorter events, 1.3 us)
Async XLA Ops:
  0.0 45.9 %copy-start = (bf16[16,2,256,128]{3,2,1,0:T(8,128)(2,1)S(1)}, bf16[16,2,256,128]{3,2,1,0:T(8,128)(2,1)}, u32[]{:S(2)}) copy-start(bf16[16,2,256,128]{3,2,1,0:T(8,128)(2,1)} %param.10) | copy-start | bytes 6291460
  2.4 23.5 %all-to-all-start.1 = ((s32[64,4,9]{2,1,0:T(4,128)}), s32[64,4,9]{2,1,0:T(4,128)S(1)}, u32[]{:S(2)}, u32[]{:S(2)}) async-start(s32[64,4,9]{2,1,0:T(4,128)} %broadcast_in_dim.23), calls=%async_computation.1 | async-start | bytes 262144 | tf_op jit(solution)/shard_map/all_to_all | solution.py:13
  17.9 2.9 %copy-start.1 = (bf16[4,8,256,128]{3,2,1,0:T(8,128)(2,1)S(1)}, bf16[4,8,256,128]{3,2,1,0:T(8,128)(2,1)}, u32[]{:S(2)}) copy-start(bf16[4,8,256,128]{3,2,1,0:T(8,128)(2,1)} %param.13) | copy-start | bytes 6291460
  25.9 8.8 %all-to-all-start.3 = ((f32[1,4,8,4,130]{4,3,1,0,2:T(4,128)}), f32[1,4,8,4,130]{4,3,1,0,2:T(4,128)S(1)}, u32[]{:S(2)}, u32[]{:S(2)}) async-start(f32[1,4,8,4,130]{4,3,1,0,2:T(4,128)} %copy.133), calls=%async_computation.3 | async-start | bytes 262144 | tf_op jit(solution)/shard_map/all_to_all | solution.py:43
  35.7 26.4 %all-to-all-start = ((bf16[64,4,1024]{2,1,0:T(4,128)(2,1)}), bf16[64,4,1024]{2,1,0:T(4,128)(2,1)S(1)}, u32[]{:S(2)}, u32[]{:S(2)}) async-start(bf16[64,4,1024]{2,1,0:T(4,128)(2,1)} %broadcast_in_dim.22), calls=%async_computation | async-start | bytes 1048576 | tf_op jit(solution)/shard_map/all_to_all | solution.py:13
  66.5 15.6 %all-to-all-start.2 = ((f32[64,1,4]{2,1,0:T(1,128)}), f32[64,1,4]{2,1,0:T(1,128)S(1)}, u32[]{:S(2)}, u32[]{:S(2)}) async-start(f32[64,1,4]{2,1,0:T(1,128)} %bitcast.13), calls=%async_computation.2 | async-start | bytes 65536 | tf_op jit(solution)/shard_map/all_to_all | solution.py:144
  82.1 14.1 %all-to-all-start.5 = ((f32[64,1,4]{2,1,0:T(1,128)}), f32[64,1,4]{2,1,0:T(1,128)S(1)}, u32[]{:S(2)}, u32[]{:S(2)}) async-start(f32[64,1,4]{2,1,0:T(1,128)} %bitcast.32), calls=%async_computation.5 | async-start | bytes 65536 | tf_op jit(solution)/shard_map/all_to_all | solution.py:145
  96.3 16.2 %all-to-all-start.4 = ((f32[64,1,4,128]{3,2,1,0:T(4,128)}), f32[64,1,4,128]{3,2,1,0:T(4,128)S(1)}, u32[]{:S(2)}, u32[]{:S(2)}) async-start(f32[64,1,4,128]{3,2,1,0:T(4,128)} %convolution_bitcast_fusion), calls=%async_computation.4 | async-start | bytes 262144 | tf_op jit(solution)/shard_map/all_to_all | solution.py:143
where the time goes:
time: 115 us; the launch traced here: 114 us
  starting transfers between devices  43 us (37%)
  waiting for transfers between devices  37.4 us (33%)
  local copies, waits for them, and re-layouts  18.9 us (16%)
  matrix products  10.9 us (9%)
  other arithmetic  3.34 us (3%)
    all_to_all x2, starting transfers between devices, sent_to_all(): return lax.all_to_all(copies, axis, split_axis=0, concat_axis=0, tiled=True)  22.2 us
    all_to_all x2, waiting for transfers between devices, sent_to_all(): return lax.all_to_all(copies, axis, split_axis=0, concat_axis=0, tiled=True)  11.8 us
    all_to_all x1, waiting for transfers between devices, per_device(): lax.all_to_all(summed, 'cache', split_axis=0, concat_axis=0, tiled=True)  9.15 us
    all_to_all x1, waiting for transfers between devices, per_device(): lax.all_to_all(highest, 'cache', split_axis=0, concat_axis=0, tiled=True)  7.69 us
    all_to_all x1, starting transfers between devices, per_device(): lax.all_to_all(highest, 'cache', split_axis=0, concat_axis=0, tiled=True)  6.29 us
    dot_general x2, matrix products, partial_attention(): jnp.einsum('rhgd,rhnd->rhgn', query_heads, key_rows, preferred_element_ty...  5.89 us
    all_to_all x1, starting transfers between devices, per_device(): lax.all_to_all(summed, 'cache', split_axis=0, concat_axis=0, tiled=True)  5.82 us
    dot_general x2, matrix products, partial_attention(): jnp.einsum('rhgn,rhnd->rhgd', exponent, value_rows.astype(jnp.float32), p...  5.05 us
  transfers between devices with their start and end apart: 6, of which 6 were waited for; matrix products, arithmetic and copies ran while one was open for 21% of the time, Pallas kernels for 0%

commit v1 on v0

v1 whole, which is shorter than its diff:
```python
import functools

import jax
import jax.numpy as jnp
from jax import lax
from jax.experimental import pallas as pl
from jax.experimental.pallas import tpu as pltpu
from jax.sharding import PartitionSpec as P

MESH = pl.DeviceIdType.MESH
NY, NZ, NC, NG = 4, 8, 2, 4
PEERS = NY * NZ * NC
ROWS, HEADS, PER_KV, TOP = 4, 2, 4, 4
KVH, HD, BLOCK = 8, 128, 128
RECENT = 256
SCALE = HD ** (-0.5)
MSG = 6
RES = 5
WANTED = ROWS * HEADS * TOP


def signed(j):
    return ((j + 1) // 2) * (2 * (j % 2) - 1)


def split_position(cache):
    return cache // (NZ * NC), cache // NC % NZ, cache % NC


def peer(cache, jz, jy, jc, sign):
    y, z, c = split_position(cache)
    ny = (y + NY + sign * signed(jy)) % NY
    nz = (z + NZ + sign * signed(jz)) % NZ
    nc = (c + jc) % NC
    return (ny * NZ + nz) * NC + nc


def slot_of(cache, owner):
    y, z, c = split_position(cache)
    oy, oz, oc = split_position(owner)
    dy, dz, dc = (oy - y + NY) % NY, (oz - z + NZ) % NZ, (oc - c + NC) % NC
    jy = jnp.where(dy == 0, 0, jnp.where(dy <= NY // 2, 2 * dy - 1, 2 * (NY - dy)))
    jz = jnp.where(dz == 0, 0, jnp.where(dz <= NZ // 2, 2 * dz - 1, 2 * (NZ - dz)))
    return (jz * NY + jy) * NC + dc


def iota(shape, dim):
    return lax.broadcasted_iota(jnp.int32, shape, dim)


def high_low(p):
    high = p.astype(jnp.bfloat16)
    low = (p - high.astype(jnp.float32)).astype(jnp.bfloat16)
    return jnp.concatenate([high, low], axis=0)


def dot_t(a, b):
    return lax.dot_general(a, b, (((1,), (1,)), ((), ())), preferred_element_type=jnp.float32)


def dot(a, b):
    return jnp.dot(a, b, preferred_element_type=jnp.float32)


def kernel(
    sel_ref, req_ref, q_ref, ck_ref, cv_ref, rk_ref, rv_ref, out_ref,
    ck, cv, rk, rv, rhs, msg_out, msg_in, res_out, res_in, near_out, near_in, far_o, far_s, slots,
    load_sem, msg_send, msg_recv, res_send, res_recv, near_send, near_recv,
):
    cache = lax.axis_index("cache")
    group = lax.axis_index("group")
    barrier = pltpu.get_barrier_semaphore()

    def each_peer(fn):
        def step(i, carry):
            j = PEERS - 1 - i
            fn(j, j // (NY * NC), j // NC % NY, j % NC)
            return carry

        lax.fori_loop(0, PEERS - 1, step, 0)

    def greet(j, jz, jy, jc):
        pl.semaphore_signal(
            barrier, inc=1, device_id=(peer(cache, jz, jy, jc, 1), group), device_id_type=MESH
        )

    each_peer(greet)
    for dg in range(1, NG):
        pl.semaphore_signal(
            barrier, inc=1, device_id=(cache, (group + dg) % NG), device_id_type=MESH
        )

    loads = [
        pltpu.make_async_copy(src, dst, load_sem.at[i])
        for i, (src, dst) in enumerate(((rk_ref, rk), (rv_ref, rv), (ck_ref, ck), (cv_ref, cv)))
    ]
    for load in loads:
        load.start()

    lane = iota((8, 128), 1)
    wanted_by = [jnp.full((8, 128), -1, jnp.int32) for _ in range(TOP)]
    codes = jnp.zeros((WANTED, 128), jnp.int32)
    code_row = iota((WANTED, 128), 0)
    for r in range(ROWS):
        prompt = req_ref[r]
        for h in range(HEADS):
            here = (lane < 32) & (lane // 16 == h) & (lane % 4 == r)
            for k in range(TOP):
                e = (r * HEADS + h) * TOP + k
                block = sel_ref[r, h, k]
                owner = block // 2
                slots[e] = slot_of(cache, owner)
                wanted_by[k] = jnp.where(here, owner, wanted_by[k])
                wanted_by[0] = jnp.where(lane == 32 + e, owner, wanted_by[0])
                codes = jnp.where(code_row == e, prompt * 4 + h * 2 + block % 2 + 1, codes)
    wanted_by = [jnp.broadcast_to(w[0:1], (64, 128)) for w in wanted_by]
    rhs[0:32, :] = q_ref[pl.ds(pl.multiple_of(group * 32, 32), 32), :]
    rhs[32:64, :] = codes.astype(jnp.float32).astype(jnp.bfloat16)
    rhs[64:128, :] = jnp.zeros((64, 128), jnp.bfloat16)
    table = rhs[...]
    row64 = iota((64, 128), 0)
    lane64 = iota((64, 128), 1)
    col_row = jnp.where(lane64 < 32, lane64 // 4 % 4, jnp.where(lane64 < 64, 4, 9))
    row_match = row64 % 8 == col_row
    y, z, c = split_position(cache)
    local = row64 // 8
    jy, jc = local // NC, local % NC
    vy = (y + NY + signed(jy)) % NY
    vc = (c + jc) % NC
    base = vy * (NZ * NC) + vc
    for jz in range(NZ):
        owner = base + ((z + NZ + signed(jz)) % NZ) * NC
        hit = wanted_by[0] == owner
        for k in range(1, TOP):
            hit = hit | (wanted_by[k] == owner)
        pick = jnp.where(hit & row_match, 1.0, 0.0).astype(jnp.bfloat16)
        msg_out[jz * 8 : (jz + 1) * 8] = dot(pick, table).reshape(8, 8, 128).astype(jnp.bfloat16)

    pl.semaphore_wait(barrier, PEERS - 1 + NG - 1)

    def message(j, jz, jy, jc):
        return pltpu.make_async_remote_copy(
            src_ref=msg_out.at[j, pl.ds(0, MSG)],
            dst_ref=msg_in.at[j, pl.ds(0, MSG)],
            send_sem=msg_send.at[j],
            recv_sem=msg_recv.at[j],
            device_id=(peer(cache, jz, jy, jc, 1), group),
            device_id_type=MESH,
        )

    each_peer(lambda *at: message(*at).start())
    own_message = pltpu.make_async_copy(
        msg_out.at[0, pl.ds(0, MSG)], msg_in.at[0, pl.ds(0, MSG)], msg_recv.at[0]
    )
    own_message.start()

    loads[0].wait()
    loads[1].wait()
    row16 = iota((16, RECENT), 0) % ROWS
    row32 = iota((32, HD), 0) % ROWS
    lane16 = iota((16, HD), 1)

    def recent(h, carry):
        x = q_ref[pl.ds(pl.multiple_of(h * 16, 16), 16), :]
        s = dot_t(x, rk[h])
        for r in range(1, ROWS):
            s = jnp.where(row16 == r, dot_t(x, rk[r * KVH + h]), s)
        s = s * SCALE
        m = jnp.max(s, axis=1, keepdims=True)
        p = jnp.exp(s - m)
        total = jnp.sum(p, axis=1, keepdims=True)
        both = high_low(p)
        o = dot(both, rv[h])
        for r in range(1, ROWS):
            o = jnp.where(row32 == r, dot(both, rv[r * KVH + h]), o)
        near_out[h, 0] = o[0:16] + o[16:32]
        near_out[h, 1] = jnp.where(lane16 < 64, m, total)
        return carry

    lax.fori_loop(0, KVH, recent, 0)

    nears = []
    for dg in range(1, NG):
        target = (group + dg) % NG
        nears.append(
            pltpu.make_async_remote_copy(
                src_ref=near_out.at[pl.ds(target * HEADS, HEADS)],
                dst_ref=near_in.at[dg],
                send_sem=near_send.at[dg],
                recv_sem=near_recv.at[dg],
                device_id=(cache, target),
                device_id_type=MESH,
            )
        )
    for near in nears:
        near.start()

    loads[2].wait()
    loads[3].wait()

    def result(j, jz, jy, jc):
        return pltpu.make_async_remote_copy(
            src_ref=res_out.at[j, pl.ds(0, RES)],
            dst_ref=res_in.at[j, pl.ds(0, RES)],
            send_sem=res_send.at[j],
            recv_sem=res_recv.at[j],
            device_id=(peer(cache, jz, jy, jc, -1), group),
            device_id_type=MESH,
        )

    own_result = pltpu.make_async_copy(
        res_out.at[0, pl.ds(0, RES)], res_in.at[0, pl.ds(0, RES)], res_recv.at[0]
    )
    row8 = iota((8, 128), 0)
    m_at = (lane == row8) & (row8 < PER_KV)
    t_at = (lane == row8 + PER_KV) & (row8 < PER_KV)

    def attend(j):
        x = msg_in[j]
        code = jnp.max(x[4:5, :].astype(jnp.float32)).astype(jnp.int32)
        block = jnp.clip(code - 1, 0, PEERS - 1)
        s = dot_t(x, ck[block]) * SCALE
        m = jnp.max(s, axis=1, keepdims=True)
        p = jnp.exp(s - m)
        total = jnp.sum(p, axis=1, keepdims=True)
        o = dot(high_low(p), cv[block])
        stat = jnp.sum(jnp.where(m_at, m, jnp.where(t_at, total, 0.0)), axis=0, keepdims=True)
        res_out[j] = jnp.where(row8 < PER_KV, o[0:8] + o[8:16], stat)

    def far(jz, first):
        for i in range(first, 8):
            message(jz * 8 + i, jz, i // NC, i % NC).wait_recv()
        if first:
            own_message.wait()
        for i in range(8):
            attend(jz * 8 + i)
        if first:
            own_result.start()
        for i in range(first, 8):
            result(jz * 8 + i, jz, i // NC, i % NC).start()

    far(0, 1)
    lax.fori_loop(1, NZ, lambda jz, carry: (far(jz, 0), carry)[1], 0)

    for near in nears:
        near.wait()
    own_result.wait()
    each_peer(lambda *at: result(*at).wait_recv())

    for r in range(ROWS):
        for h in range(HEADS):
            for k in range(TOP):
                e = (r * HEADS + h) * TOP + k
                tile = res_in[slots[e]]
                rows = pl.ds(h * 16 + r, 4, stride=4)
                far_o[k, rows, :] = tile[0:4]
                far_s[k, rows, :] = jnp.broadcast_to(tile[4:5], (4, 128))
    lane32 = iota((32, 128), 1)
    which = iota((32, 128), 0) // 4 % 4
    parts = []
    for k in range(TOP):
        stat = far_s[k]
        m = jnp.sum(jnp.where(lane32 == which, stat, 0.0), axis=1, keepdims=True)
        total = jnp.sum(jnp.where(lane32 == which + PER_KV, stat, 0.0), axis=1, keepdims=True)
        parts.append((far_o[k], m, total))
    for dg in range(NG):
        if dg:
            both = near_in[dg]
        else:
            both = near_out[pl.ds(group * HEADS, HEADS)]
        stat = both[:, 1].reshape(32, 128)
        parts.append((both[:, 0].reshape(32, 128), stat[:, 0:1], stat[:, 64:65]))
    peak = functools.reduce(jnp.maximum, [m for _, m, _ in parts])
    summed, weight = 0.0, 0.0
    for o, m, total in parts:
        factor = jnp.exp(m - peak)
        summed = summed + factor * o
        weight = weight + factor * total
    out_ref[...] = (summed / weight).astype(out_ref.dtype)

    each_peer(lambda *at: message(*at).wait_send())
    each_peer(lambda *at: result(*at).wait_send())


def per_device(queries, request_of, selected, cache_keys, cache_values, recent_keys, recent_values):
    q = queries.reshape(ROWS, KVH * PER_KV, HD).transpose(1, 0, 2).reshape(128, HD)
    blocks = lambda a: a.reshape(PEERS, BLOCK, HD)
    recents = lambda a: a.reshape(ROWS * KVH, RECENT, HD)
    vmem = lambda shape, kind: pltpu.VMEM(shape, kind)
    dma = pltpu.SemaphoreType.DMA
    bf16, f32 = jnp.bfloat16, jnp.float32
    out = pl.pallas_call(
        kernel,
        out_shape=jax.ShapeDtypeStruct((32, HD), bf16),
        in_specs=[pl.BlockSpec(memory_space=pltpu.SMEM)] * 2
        + [pl.BlockSpec(memory_space=pltpu.VMEM)]
        + [pl.BlockSpec(memory_space=pltpu.HBM)] * 4,
        out_specs=pl.BlockSpec(memory_space=pltpu.VMEM),
        scratch_shapes=[
            vmem((PEERS, BLOCK, HD), bf16),
            vmem((PEERS, BLOCK, HD), bf16),
            vmem((ROWS * KVH, RECENT, HD), bf16),
            vmem((ROWS * KVH, RECENT, HD), bf16),
            vmem((128, HD), bf16),
            vmem((PEERS, 8, HD), bf16),
            vmem((PEERS, 8, HD), bf16),
            vmem((PEERS, 8, HD), f32),
            vmem((PEERS, 8, HD), f32),
            vmem((KVH, 2, 16, HD), f32),
            vmem((NG, HEADS, 2, 16, HD), f32),
            vmem((TOP, 32, HD), f32),
            vmem((TOP, 32, HD), f32),
            pltpu.SMEM((WANTED,), jnp.int32),
            dma((4,)),
            dma((PEERS,)),
            dma((PEERS,)),
            dma((PEERS,)),
            dma((PEERS,)),
            dma((NG,)),
            dma((NG,)),
        ],
        compiler_params=pltpu.CompilerParams(
            collective_id=0, has_side_effects=True, vmem_limit_bytes=40 * 1024 * 1024
        ),
    )(
        selected, request_of, q, blocks(cache_keys), blocks(cache_values),
        recents(recent_keys), recents(recent_values),
    )
    return out.reshape(HEADS * PER_KV, ROWS, HD).transpose(1, 0, 2).reshape(ROWS, HEADS * PER_KV * HD)


def solution(mesh):
    return jax.shard_map(
        per_device,
        mesh=mesh,
        in_specs=(
            P("cache", None),
            P("cache"),
            P("cache", "group", None),
            P(None, "group", "cache", None),
            P(None, "group", "cache", None),
            P("cache", None, "group", None),
            P("cache", None, "group", None),
        ),
        out_specs=P("cache", "group"),
        check_vma=False,
    )
```

time: 115 us -> 56.4 us (0.49)
  Pallas kernels: 0 us -> 47 us
  starting transfers between devices: 43 us -> 0 us
  waiting for transfers between devices: 37.4 us -> 0 us
  matrix products: 10.9 us -> 0 us
  local copies, waits for them, and re-layouts: 18.9 us -> 9.06 us
  other arithmetic: 3.34 us -> 0 us
    pallas_call x0 -> x1, Pallas kernels: none -> 47 us  [per_device(): pl.pallas_call(kernel, out_shape=jax.ShapeDtypeStruct((32, HD), bf16), in...]
    all_to_all x6 -> x0, starting transfers between devices: 43 us -> none  [the longest x2 22.2 us: sent_to_all(): return lax.all_to_all(copies, axis, split_axis=0, concat_axis=0, tiled=True)]
    all_to_all x6 -> x0, waiting for transfers between devices: 37.4 us -> none  [the longest x2 11.8 us: sent_to_all(): return lax.all_to_all(copies, axis, split_axis=0, concat_axis=0, tiled=True)]
    dot_general x4 -> x0, matrix products: 10.9 us -> none  [the longest x2 5.89 us: partial_attention(): jnp.einsum('rhgd,rhnd->rhgn', query_heads, key_rows, preferred_element_ty...]
    gather x7 -> x0, local copies, waits for them, and re-layouts: 9.43 us -> none  [the longest x1 3.82 us: owner_plan(): cache_values.reshape(cache_values.shape[0], mine_heads, per_owner, BLOCK,...]
    unnamed x5 -> x15, local copies, waits for them, and re-layouts: 0.01 us -> 9.06 us
    reshape x10 -> x0, local copies, waits for them, and re-layouts: 4.62 us -> none  [the longest x2 1.66 us: in_one_piece(): columns = [a.reshape(*a.shape[:along], -1) for a in arrays]]
    reduce_sum x6 -> x0, other arithmetic: 2.48 us -> none  [the longest x2 1.84 us: partial_attention(): totals = jnp.sum(exponent, axis=-1)]
  transfers between devices with their start and end apart: 6 -> 0, of which waited for: 6 -> 0; matrix products, arithmetic and copies ran while one was open for 21% -> 0% of each run, Pallas kernels for 0% -> 0%
where the time goes in v1:
time: 56.4 us; the launch traced here: 56.1 us
  Pallas kernels  47 us (83%)
  local copies, waits for them, and re-layouts  9.06 us (16%)
    pallas_call x1, Pallas kernels, per_device(): pl.pallas_call(kernel, out_shape=jax.ShapeDtypeStruct((32, HD), bf16), in...  47 us
    unnamed x15, local copies, waits for them, and re-layouts  9.06 us

profile of v1, /device:TPU:1, one launch (start us, length us, event | category | flops | bytes accessed | tf_op | source)
XLA Modules:
  0.0 56.1 jit_solution(1033498155681509921)
XLA Ops:
  0.0 0.0 copy-start
  0.0 1.6 %copy-done = bf16[16,2,256,128]{3,2,1,0:T(8,128)(2,1)S(1)} copy-done((bf16[16,2,256,128]{3,2,1,0:T(8,128)(2,1)S(1)}, bf16[16,2,256,128]{3,2,1,0:T(8,128)(2,1)}, u32[]{:S(2)}) %copy-start) | copy-done | bytes 2097176
  1.6 0.0 copy-start.1
  1.6 1.6 %copy-done.1 = bf16[16,2,256,128]{3,2,1,0:T(8,128)(2,1)S(1)} copy-done((bf16[16,2,256,128]{3,2,1,0:T(8,128)(2,1)S(1)}, bf16[16,2,256,128]{3,2,1,0:T(8,128)(2,1)}, u32[]{:S(2)}) %copy-start.1) | copy-done | bytes 2097176
  3.2 0.0 copy-start.2
  3.2 1.6 %copy-done.2 = bf16[4,8,256,128]{3,2,1,0:T(8,128)(2,1)S(1)} copy-done((bf16[4,8,256,128]{3,2,1,0:T(8,128)(2,1)S(1)}, bf16[4,8,256,128]{3,2,1,0:T(8,128)(2,1)}, u32[]{:S(2)}) %copy-start.2) | copy-done | bytes 2097176
  4.8 0.0 copy-start.3
  4.8 1.6 %copy-done.3 = bf16[4,8,256,128]{3,2,1,0:T(8,128)(2,1)S(1)} copy-done((bf16[4,8,256,128]{3,2,1,0:T(8,128)(2,1)S(1)}, bf16[4,8,256,128]{3,2,1,0:T(8,128)(2,1)}, u32[]{:S(2)}) %copy-start.3) | copy-done | bytes 2097176
  6.4 0.0 copy-start.4
  6.4 0.8 %copy-done.4 = bf16[4,4096]{1,0:T(4,128)(2,1)S(1)} copy-done((bf16[4,4096]{1,0:T(4,128)(2,1)S(1)}, bf16[4,4096]{1,0:T(4,128)(2,1)}, u32[]{:S(2)}) %copy-start.4) | copy-done | bytes 32792
  7.1 0.0 copy-start.5
  7.1 0.7 %copy-done.5 = s32[4,2,4]{2,1,0:T(2,128)S(1)} copy-done((s32[4,2,4]{2,1,0:T(2,128)S(1)}, s32[4,2,4]{2,1,0:T(2,128)}, u32[]{:S(2)}) %copy-start.5) | copy-done | bytes 152
  7.8 0.0 copy-start.6
  7.8 0.7 %copy-done.6 = s32[4]{0:T(128)S(1)} copy-done((s32[4]{0:T(128)S(1)}, s32[4]{0:T(128)}, u32[]{:S(2)}) %copy-start.6) | copy-done | bytes 40
  8.5 47.0 %shard_map.73 = bf16[32,128]{1,0:T(8,128)(2,1)S(1)} custom-call(s32[4,2,4]{2,1,0:T(2,128)S(1)} %copy-done.5, s32[4]{0:T(128)S(1)} %copy-done.6, bf16[128,128]{1,0:T(8,128)(2,1)S(1)} %bitcast.18, bf16[64,128,128]{2,1,0:T(8,128)(2,1)S(1)} %bitcast.14, bf16[64,128,128]{2,1,0:T(8,128)(2,1)S(1)} %bitcast.15, bf16[32,256,128]{2,1,0:T(8,128)(2,1)S(1)} %bitcast.16, ...), custom_call_target="tpu_custom_call" | custom-call | tf_op jit(solution)/shard_map/pallas_call | solution.py:292
  55.5 0.6 %copy.11 = bf16[4,1024]{1,0:T(4,128)(2,1)} copy(bf16[4,1024]{1,0:T(4,128)(2,1)S(1)} %bitcast.19) | data formatting | bytes 16384
Async XLA Ops:
  0.0 1.6 %copy-start = (bf16[16,2,256,128]{3,2,1,0:T(8,128)(2,1)S(1)}, bf16[16,2,256,128]{3,2,1,0:T(8,128)(2,1)}, u32[]{:S(2)}) copy-start(bf16[16,2,256,128]{3,2,1,0:T(8,128)(2,1)} %param.10) | copy-start | bytes 6291460
  1.6 1.6 %copy-start.1 = (bf16[16,2,256,128]{3,2,1,0:T(8,128)(2,1)S(1)}, bf16[16,2,256,128]{3,2,1,0:T(8,128)(2,1)}, u32[]{:S(2)}) copy-start(bf16[16,2,256,128]{3,2,1,0:T(8,128)(2,1)} %param.11) | copy-start | bytes 6291460
  3.2 1.6 %copy-start.2 = (bf16[4,8,256,128]{3,2,1,0:T(8,128)(2,1)S(1)}, bf16[4,8,256,128]{3,2,1,0:T(8,128)(2,1)}, u32[]{:S(2)}) copy-start(bf16[4,8,256,128]{3,2,1,0:T(8,128)(2,1)} %param.12) | copy-start | bytes 6291460
  4.8 1.6 %copy-start.3 = (bf16[4,8,256,128]{3,2,1,0:T(8,128)(2,1)S(1)}, bf16[4,8,256,128]{3,2,1,0:T(8,128)(2,1)}, u32[]{:S(2)}) copy-start(bf16[4,8,256,128]{3,2,1,0:T(8,128)(2,1)} %param.13) | copy-start | bytes 6291460
  6.4 0.8 %copy-start.4 = (bf16[4,4096]{1,0:T(4,128)(2,1)S(1)}, bf16[4,4096]{1,0:T(4,128)(2,1)}, u32[]{:S(2)}) copy-start(bf16[4,4096]{1,0:T(4,128)(2,1)} %param.7) | copy-start | bytes 98308
  7.1 0.7 %copy-start.5 = (s32[4,2,4]{2,1,0:T(2,128)S(1)}, s32[4,2,4]{2,1,0:T(2,128)}, u32[]{:S(2)}) copy-start(s32[4,2,4]{2,1,0:T(2,128)} %sel_ref.1) | copy-start | bytes 388
  7.8 0.7 %copy-start.6 = (s32[4]{0:T(128)S(1)}, s32[4]{0:T(128)}, u32[]{:S(2)}) copy-start(s32[4]{0:T(128)} %req_ref.1) | copy-start | bytes 52

commit v2 on v1

--- a/solution.py
+++ b/solution.py
@@ -23,27 +23,6 @@
     return ((j + 1) // 2) * (2 * (j % 2) - 1)
 
 
-def split_position(cache):
-    return cache // (NZ * NC), cache // NC % NZ, cache % NC
-
-
-def peer(cache, jz, jy, jc, sign):
-    y, z, c = split_position(cache)
-    ny = (y + NY + sign * signed(jy)) % NY
-    nz = (z + NZ + sign * signed(jz)) % NZ
-    nc = (c + jc) % NC
-    return (ny * NZ + nz) * NC + nc
-
-
-def slot_of(cache, owner):
-    y, z, c = split_position(cache)
-    oy, oz, oc = split_position(owner)
-    dy, dz, dc = (oy - y + NY) % NY, (oz - z + NZ) % NZ, (oc - c + NC) % NC
-    jy = jnp.where(dy == 0, 0, jnp.where(dy <= NY // 2, 2 * dy - 1, 2 * (NY - dy)))
-    jz = jnp.where(dz == 0, 0, jnp.where(dz <= NZ // 2, 2 * dz - 1, 2 * (NZ - dz)))
-    return (jz * NY + jy) * NC + dc
-
-
 def iota(shape, dim):
     return lax.broadcasted_iota(jnp.int32, shape, dim)
 
@@ -63,36 +42,42 @@
 
 
 def kernel(
-    sel_ref, req_ref, q_ref, ck_ref, cv_ref, rk_ref, rv_ref, out_ref,
-    ck, cv, rk, rv, rhs, msg_out, msg_in, res_out, res_in, near_out, near_in, far_o, far_s, slots,
+    sel_ref, req_ref, q_hbm, ck_ref, cv_ref, rk_ref, rv_ref, out_ref,
+    q_ref, ck, cv, rk, rv, rhs, msg_out, msg_in, res_out, res_in, near_out, near_in, far_o, far_s,
     load_sem, msg_send, msg_recv, res_send, res_recv, near_send, near_recv,
 ):
     cache = lax.axis_index("cache")
     group = lax.axis_index("group")
+    y = lax.div(cache, NZ * NC)
+    z = lax.rem(lax.div(cache, NC), NZ)
+    c = lax.rem(cache, NC)
+    other_z = [lax.rem(z + (NZ + signed(jz)), NZ) * NC for jz in range(NZ)]
+    other_y = [lax.rem(y + (NY + signed(jy)), NY) * (NZ * NC) for jy in range(NY)]
+    other_c = [c, 1 - c]
+    other_yc = [other_y[i // NC] + other_c[i % NC] for i in range(NY * NC)]
+    opposite = lambda j, n: 0 if j == 0 else (j + 1 if j % 2 and j + 1 < n else j if j % 2 else j - 1)
+
+    def ahead(j):
+        return (other_z[j // 8] + other_yc[j % 8], group)
+
+    def behind(j):
+        jz, jy, jc = opposite(j // 8, NZ), opposite(j // NC % NY, NY), j % NC
+        return (other_z[jz] + other_yc[jy * NC + jc], group)
+
     barrier = pltpu.get_barrier_semaphore()
-
-    def each_peer(fn):
-        def step(i, carry):
-            j = PEERS - 1 - i
-            fn(j, j // (NY * NC), j // NC % NY, j % NC)
-            return carry
-
-        lax.fori_loop(0, PEERS - 1, step, 0)
-
-    def greet(j, jz, jy, jc):
-        pl.semaphore_signal(
-            barrier, inc=1, device_id=(peer(cache, jz, jy, jc, 1), group), device_id_type=MESH
-        )
-
-    each_peer(greet)
+    order = range(PEERS - 1, 0, -1)
+    for j in order:
+        pl.semaphore_signal(barrier, inc=1, device_id=ahead(j), device_id_type=MESH)
     for dg in range(1, NG):
         pl.semaphore_signal(
-            barrier, inc=1, device_id=(cache, (group + dg) % NG), device_id_type=MESH
+            barrier, inc=1, device_id=(cache, lax.rem(group + dg, NG)), device_id_type=MESH
         )
 
     loads = [
         pltpu.make_async_copy(src, dst, load_sem.at[i])
-        for i, (src, dst) in enumerate(((rk_ref, rk), (rv_ref, rv), (ck_ref, ck), (cv_ref, cv)))
+        for i, (src, dst) in enumerate(
+            ((q_hbm, q_ref), (rk_ref, rk), (rv_ref, rv), (ck_ref, ck), (cv_ref, cv))
+        )
     ]
     for load in loads:
         load.start()
@@ -108,28 +93,28 @@
             for k in range(TOP):
                 e = (r * HEADS + h) * TOP + k
                 block = sel_ref[r, h, k]
-                owner = block // 2
-                slots[e] = slot_of(cache, owner)
+                owner = lax.div(block, 2)
                 wanted_by[k] = jnp.where(here, owner, wanted_by[k])
                 wanted_by[0] = jnp.where(lane == 32 + e, owner, wanted_by[0])
-                codes = jnp.where(code_row == e, prompt * 4 + h * 2 + block % 2 + 1, codes)
+                code = prompt * 4 + h * 2 + (block - owner * 2) + 1
+                codes = jnp.where(code_row == e, code, codes)
     wanted_by = [jnp.broadcast_to(w[0:1], (64, 128)) for w in wanted_by]
+    loads[0].wait()
     rhs[0:32, :] = q_ref[pl.ds(pl.multiple_of(group * 32, 32), 32), :]
     rhs[32:64, :] = codes.astype(jnp.float32).astype(jnp.bfloat16)
     rhs[64:128, :] = jnp.zeros((64, 128), jnp.bfloat16)
     table = rhs[...]
     row64 = iota((64, 128), 0)
     lane64 = iota((64, 128), 1)
-    col_row = jnp.where(lane64 < 32, lane64 // 4 % 4, jnp.where(lane64 < 64, 4, 9))
-    row_match = row64 % 8 == col_row
-    y, z, c = split_position(cache)
-    local = row64 // 8
-    jy, jc = local // NC, local % NC
-    vy = (y + NY + signed(jy)) % NY
-    vc = (c + jc) % NC
-    base = vy * (NZ * NC) + vc
+    half = row64 // 8 % 2
+    place = row64 % 8
+    col_row = jnp.where(lane64 < 32, lane64 // 4 % 4 + 4 * half, jnp.where(lane64 < 64, 4 - half, 9))
+    row_match = place == col_row
+    base = jnp.zeros((64, 128), jnp.int32)
+    for i in range(8):
+        base = jnp.where(row64 // 8 == i, other_yc[i], base)
     for jz in range(NZ):
-        owner = base + ((z + NZ + signed(jz)) % NZ) * NC
+        owner = base + other_z[jz]
         hit = wanted_by[0] == owner
         for k in range(1, TOP):
             hit = hit | (wanted_by[k] == owner)
@@ -138,24 +123,26 @@
 
     pl.semaphore_wait(barrier, PEERS - 1 + NG - 1)
 
-    def message(j, jz, jy, jc):
+    def message(j):
+        at = pl.ds(0, MSG) if j % 2 == 0 else pl.ds(8 - MSG, MSG)
         return pltpu.make_async_remote_copy(
-            src_ref=msg_out.at[j, pl.ds(0, MSG)],
-            dst_ref=msg_in.at[j, pl.ds(0, MSG)],
+            src_ref=msg_out.at[j, at],
+            dst_ref=msg_in.at[j, at],
             send_sem=msg_send.at[j],
             recv_sem=msg_recv.at[j],
-            device_id=(peer(cache, jz, jy, jc, 1), group),
+            device_id=ahead(j),
             device_id_type=MESH,
         )
 
-    each_peer(lambda *at: message(*at).start())
+    for j in order:
+        message(j).start()
     own_message = pltpu.make_async_copy(
         msg_out.at[0, pl.ds(0, MSG)], msg_in.at[0, pl.ds(0, MSG)], msg_recv.at[0]
     )
     own_message.start()
 
-    loads[0].wait()
     loads[1].wait()
+    loads[2].wait()
     row16 = iota((16, RECENT), 0) % ROWS
     row32 = iota((32, HD), 0) % ROWS
     lane16 = iota((16, HD), 1)
@@ -181,7 +168,7 @@
 
     nears = []
     for dg in range(1, NG):
-        target = (group + dg) % NG
+        target = lax.rem(group + dg, NG)
         nears.append(
             pltpu.make_async_remote_copy(
                 src_ref=near_out.at[pl.ds(target * HEADS, HEADS)],
@@ -195,16 +182,16 @@
     for near in nears:
         near.start()
 
-    loads[2].wait()
     loads[3].wait()
-
-    def result(j, jz, jy, jc):
+    loads[4].wait()
+
+    def result(j):
         return pltpu.make_async_remote_copy(
             src_ref=res_out.at[j, pl.ds(0, RES)],
             dst_ref=res_in.at[j, pl.ds(0, RES)],
             send_sem=res_send.at[j],
             recv_sem=res_recv.at[j],
-            device_id=(peer(cache, jz, jy, jc, -1), group),
+            device_id=behind(j),
             device_id_type=MESH,
         )
 
@@ -212,40 +199,73 @@
         res_out.at[0, pl.ds(0, RES)], res_in.at[0, pl.ds(0, RES)], res_recv.at[0]
     )
     row8 = iota((8, 128), 0)
-    m_at = (lane == row8) & (row8 < PER_KV)
-    t_at = (lane == row8 + PER_KV) & (row8 < PER_KV)
-
-    def attend(j):
-        x = msg_in[j]
-        code = jnp.max(x[4:5, :].astype(jnp.float32)).astype(jnp.int32)
-        block = jnp.clip(code - 1, 0, PEERS - 1)
-        s = dot_t(x, ck[block]) * SCALE
-        m = jnp.max(s, axis=1, keepdims=True)
-        p = jnp.exp(s - m)
-        total = jnp.sum(p, axis=1, keepdims=True)
-        o = dot(high_low(p), cv[block])
-        stat = jnp.sum(jnp.where(m_at, m, jnp.where(t_at, total, 0.0)), axis=0, keepdims=True)
-        res_out[j] = jnp.where(row8 < PER_KV, o[0:8] + o[8:16], stat)
-
-    def far(jz, first):
-        for i in range(first, 8):
-            message(jz * 8 + i, jz, i // NC, i % NC).wait_recv()
-        if first:
-            own_message.wait()
+    upper = row8 < PER_KV
+    upper_x = iota((8, 128), 0) < PER_KV
+    m_first = upper & (lane == row8)
+    t_first = upper & (lane == row8 + PER_KV)
+    m_second = (~upper) & (lane == row8 - PER_KV)
+    t_second = (~upper) & (lane == row8)
+
+    def block_of(x, row):
+        code = x[row : row + 1, :].astype(jnp.float32)[0, 0].astype(jnp.int32)
+        return jnp.clip(code - 1, 0, PEERS - 1)
+
+    def far(jz):
+        pairs = []
+        for i in range(0, 8, 2):
+            first, second = msg_in[jz * 8 + i], msg_in[jz * 8 + i + 1]
+            a, b = block_of(first, 4), block_of(second, 3)
+            x = jnp.where(upper_x, first.astype(jnp.float32), second.astype(jnp.float32))
+            pairs.append((x.astype(jnp.bfloat16), a, b))
+        scores = []
+        for x, a, b in pairs:
+            s = dot_t(x, jnp.concatenate([ck[a], ck[b]], axis=0))
+            scores.append(jnp.where(upper, s[:, :BLOCK], s[:, BLOCK:]) * SCALE)
+        highs = [jnp.max(s, axis=1, keepdims=True) for s in scores]
+        weights = [jnp.exp(s - m) for s, m in zip(scores, highs)]
+        totals = [jnp.sum(p, axis=1, keepdims=True) for p in weights]
+        for n, ((x, a, b), p, m, t) in enumerate(zip(pairs, weights, highs, totals)):
+            both = high_low(
+                jnp.concatenate([jnp.where(upper, p, 0.0), jnp.where(upper, 0.0, p)], axis=1)
+            )
+            o = dot(both, jnp.concatenate([cv[a], cv[b]], axis=0))
+            o = o[0:8] + o[8:16]
+            one = jnp.sum(jnp.where(m_first, m, jnp.where(t_first, t, 0.0)), axis=0, keepdims=True)
+            two = jnp.sum(jnp.where(m_second, m, jnp.where(t_second, t, 0.0)), axis=0, keepdims=True)
+            res_out[jz * 8 + 2 * n] = jnp.where(upper, o, one)
+            res_out[jz * 8 + 2 * n + 1] = jnp.where(upper, pltpu.roll(o, PER_KV, 0), two)
+
+    for jz in range(NZ):
         for i in range(8):
-            attend(jz * 8 + i)
-        if first:
-            own_result.start()
-        for i in range(first, 8):
-            result(jz * 8 + i, jz, i // NC, i % NC).start()
-
-    far(0, 1)
-    lax.fori_loop(1, NZ, lambda jz, carry: (far(jz, 0), carry)[1], 0)
+            if jz + i:
+                message(jz * 8 + i).wait_recv()
+            else:
+                own_message.wait()
+        far(jz)
+        for i in range(8):
+            if jz + i:
+                result(jz * 8 + i).start()
+            else:
+                own_result.start()
+
+    slots = []
+    for r in range(ROWS):
+        for h in range(HEADS):
+            for k in range(TOP):
+                owner = lax.div(sel_ref[r, h, k], 2)
+                oy = lax.div(owner, NZ * NC)
+                oz = lax.rem(lax.div(owner, NC), NZ)
+                dc = lax.rem(owner + c, NC)
+                dy, dz = lax.rem(oy - y + NY, NY), lax.rem(oz - z + NZ, NZ)
+                jy = jnp.where(dy == 0, 0, jnp.where(dy <= NY // 2, 2 * dy - 1, 2 * (NY - dy)))
+                jz = jnp.where(dz == 0, 0, jnp.where(dz <= NZ // 2, 2 * dz - 1, 2 * (NZ - dz)))
+                slots.append((jz * NY + jy) * NC + dc)
 
     for near in nears:
         near.wait()
     own_result.wait()
-    each_peer(lambda *at: result(*at).wait_recv())
+    for j in order:
+        result(j).wait_recv()
 
     for r in range(ROWS):
         for h in range(HEADS):
@@ -278,8 +298,10 @@
         weight = weight + factor * total
     out_ref[...] = (summed / weight).astype(out_ref.dtype)
 
-    each_peer(lambda *at: message(*at).wait_send())
-    each_peer(lambda *at: result(*at).wait_send())
+    for j in order:
+        message(j).wait_send()
+    for j in order:
+        result(j).wait_send()
 
 
 def per_device(queries, request_of, selected, cache_keys, cache_values, recent_keys, recent_values):
@@ -293,10 +315,10 @@
         kernel,
         out_shape=jax.ShapeDtypeStruct((32, HD), bf16),
         in_specs=[pl.BlockSpec(memory_space=pltpu.SMEM)] * 2
-        + [pl.BlockSpec(memory_space=pltpu.VMEM)]
-        + [pl.BlockSpec(memory_space=pltpu.HBM)] * 4,
+        + [pl.BlockSpec(memory_space=pltpu.HBM)] * 5,
         out_specs=pl.BlockSpec(memory_space=pltpu.VMEM),
         scratch_shapes=[
+            vmem((128, HD), bf16),
             vmem((PEERS, BLOCK, HD), bf16),
             vmem((PEERS, BLOCK, HD), bf16),
             vmem((ROWS * KVH, RECENT, HD), bf16),
@@ -310,8 +332,7 @@
             vmem((NG, HEADS, 2, 16, HD), f32),
             vmem((TOP, 32, HD), f32),
             vmem((TOP, 32, HD), f32),
-            pltpu.SMEM((WANTED,), jnp.int32),
-            dma((4,)),
+            dma((5,)),
             dma((PEERS,)),
             dma((PEERS,)),
             dma((PEERS,)),
@@ -320,7 +341,7 @@
             dma((NG,)),
         ],
         compiler_params=pltpu.CompilerParams(
-            collective_id=0, has_side_effects=True, vmem_limit_bytes=40 * 1024 * 1024
+            collective_id=0, has_side_effects=True, vmem_limit_bytes=67043328
         ),
     )(
         selected, request_of, q, blocks(cache_keys), blocks(cache_values),

time: 56.4 us -> 32.1 us (0.57)
  Pallas kernels: 47 us -> 30.6 us
  local copies, waits for them, and re-layouts: 9.06 us -> 1.3 us
    pallas_call x1, Pallas kernels: 47 us -> 30.6 us  [per_device(): pl.pallas_call(kernel, out_shape=jax.ShapeDtypeStruct((32, HD), bf16), in...]
    unnamed x15 -> x1, local copies, waits for them, and re-layouts: 9.06 us -> 1.3 us
where the time goes in v2:
time: 32.1 us; the launch traced here: 31.9 us
  Pallas kernels  30.6 us (95%)
  local copies, waits for them, and re-layouts  1.3 us (4%)
    pallas_call x1, Pallas kernels, per_device(): pl.pallas_call(kernel, out_shape=jax.ShapeDtypeStruct((32, HD), bf16), in...  30.6 us
    unnamed x1, local copies, waits for them, and re-layouts  1.3 us

profile of v2, /device:TPU:1, one launch (start us, length us, event | category | flops | bytes accessed | tf_op | source)
XLA Modules:
  0.0 31.9 jit_solution(8095109867744587797)
XLA Ops:
  0.0 30.6 %shard_map.73 = bf16[32,128]{1,0:T(8,128)(2,1)} custom-call(s32[4,2,4]{2,1,0:T(2,128)} %sel_ref.1, s32[4]{0:T(128)} %req_ref.1, bf16[128,128]{1,0:T(8,128)(2,1)} %bitcast.18, bf16[64,128,128]{2,1,0:T(8,128)(2,1)} %bitcast.14, bf16[64,128,128]{2,1,0:T(8,128)(2,1)} %bitcast.15, bf16[32,256,128]{2,1,0:T(8,128)(2,1)} %bitcast.16, bf16[32,256,128]{2,1,0:T(8,128)(2,1)} %bitcast.17), custom_call_target="tpu_custom_call" | custom-call | tf_op jit(solution)/shard_map/pallas_call | solution.py:314
  30.6 1.3 %copy.11 = bf16[4,1024]{1,0:T(4,128)(2,1)} copy(bf16[4,1024]{1,0:T(4,128)(2,1)} %bitcast.19) | data formatting | bytes 16384

commit v3 on v2

--- a/solution.py
+++ b/solution.py
@@ -42,9 +42,9 @@
 
 
 def kernel(
-    sel_ref, req_ref, q_hbm, ck_ref, cv_ref, rk_ref, rv_ref, out_ref,
-    q_ref, ck, cv, rk, rv, rhs, msg_out, msg_in, res_out, res_in, near_out, near_in, far_o, far_s,
-    load_sem, msg_send, msg_recv, res_send, res_recv, near_send, near_recv,
+    sel_hbm, req_hbm, q_hbm, ck_ref, cv_ref, rk_ref, rv_ref, out_hbm,
+    sel_ref, req_ref, out_ref, q_ref, ck, cv, rk, rv, rhs, msg_out, msg_in, res_out, res_in, near_out, near_in, far_o, far_s,
+    load_sem, out_sem, msg_send, msg_recv, res_send, res_recv, near_send, near_recv,
 ):
     cache = lax.axis_index("cache")
     group = lax.axis_index("group")
@@ -76,11 +76,17 @@
     loads = [
         pltpu.make_async_copy(src, dst, load_sem.at[i])
         for i, (src, dst) in enumerate(
-            ((q_hbm, q_ref), (rk_ref, rk), (rv_ref, rv), (ck_ref, ck), (cv_ref, cv))
+            (
+                (sel_hbm, sel_ref), (req_hbm, req_ref), (q_hbm, q_ref),
+                (rk_ref, rk), (rv_ref, rv), (ck_ref, ck), (cv_ref, cv),
+            )
         )
     ]
     for load in loads:
         load.start()
+
+    loads[0].wait()
+    loads[1].wait()
 
     lane = iota((8, 128), 1)
     wanted_by = [jnp.full((8, 128), -1, jnp.int32) for _ in range(TOP)]
@@ -99,7 +105,7 @@
                 code = prompt * 4 + h * 2 + (block - owner * 2) + 1
                 codes = jnp.where(code_row == e, code, codes)
     wanted_by = [jnp.broadcast_to(w[0:1], (64, 128)) for w in wanted_by]
-    loads[0].wait()
+    loads[2].wait()
     rhs[0:32, :] = q_ref[pl.ds(pl.multiple_of(group * 32, 32), 32), :]
     rhs[32:64, :] = codes.astype(jnp.float32).astype(jnp.bfloat16)
     rhs[64:128, :] = jnp.zeros((64, 128), jnp.bfloat16)
@@ -128,8 +134,8 @@
         return pltpu.make_async_remote_copy(
             src_ref=msg_out.at[j, at],
             dst_ref=msg_in.at[j, at],
-            send_sem=msg_send.at[j],
-            recv_sem=msg_recv.at[j],
+            send_sem=msg_send,
+            recv_sem=msg_recv.at[j // 8],
             device_id=ahead(j),
             device_id_type=MESH,
         )
@@ -141,8 +147,21 @@
     )
     own_message.start()
 
-    loads[1].wait()
-    loads[2].wait()
+    slots = []
+    for r in range(ROWS):
+        for h in range(HEADS):
+            for k in range(TOP):
+                owner = lax.div(sel_ref[r, h, k], 2)
+                oy = lax.div(owner, NZ * NC)
+                oz = lax.rem(lax.div(owner, NC), NZ)
+                dc = lax.rem(owner + c, NC)
+                dy, dz = lax.rem(oy - y + NY, NY), lax.rem(oz - z + NZ, NZ)
+                jy = jnp.where(dy == 0, 0, jnp.where(dy <= NY // 2, 2 * dy - 1, 2 * (NY - dy)))
+                jz = jnp.where(dz == 0, 0, jnp.where(dz <= NZ // 2, 2 * dz - 1, 2 * (NZ - dz)))
+                slots.append((jz * NY + jy) * NC + dc)
+
+    loads[3].wait()
+    loads[4].wait()
     row16 = iota((16, RECENT), 0) % ROWS
     row32 = iota((32, HD), 0) % ROWS
     lane16 = iota((16, HD), 1)
@@ -182,25 +201,24 @@
     for near in nears:
         near.start()
 
-    loads[3].wait()
-    loads[4].wait()
+    loads[5].wait()
+    loads[6].wait()
 
     def result(j):
         return pltpu.make_async_remote_copy(
             src_ref=res_out.at[j, pl.ds(0, RES)],
             dst_ref=res_in.at[j, pl.ds(0, RES)],
-            send_sem=res_send.at[j],
-            recv_sem=res_recv.at[j],
+            send_sem=res_send,
+            recv_sem=res_recv,
             device_id=behind(j),
             device_id_type=MESH,
         )
 
     own_result = pltpu.make_async_copy(
-        res_out.at[0, pl.ds(0, RES)], res_in.at[0, pl.ds(0, RES)], res_recv.at[0]
+        res_out.at[0, pl.ds(0, RES)], res_in.at[0, pl.ds(0, RES)], res_recv
     )
     row8 = iota((8, 128), 0)
     upper = row8 < PER_KV
-    upper_x = iota((8, 128), 0) < PER_KV
     m_first = upper & (lane == row8)
     t_first = upper & (lane == row8 + PER_KV)
     m_second = (~upper) & (lane == row8 - PER_KV)
@@ -210,21 +228,30 @@
         code = x[row : row + 1, :].astype(jnp.float32)[0, 0].astype(jnp.int32)
         return jnp.clip(code - 1, 0, PEERS - 1)
 
-    def far(jz):
+    def scores_of(jz):
+        msgs = pl.ds(jz * 8, 8)
+        pltpu.make_async_copy(
+            msg_out.at[msgs, pl.ds(0, MSG)], msg_in.at[msgs, pl.ds(0, MSG)], msg_recv.at[jz]
+        ).wait()
         pairs = []
         for i in range(0, 8, 2):
             first, second = msg_in[jz * 8 + i], msg_in[jz * 8 + i + 1]
             a, b = block_of(first, 4), block_of(second, 3)
-            x = jnp.where(upper_x, first.astype(jnp.float32), second.astype(jnp.float32))
+            x = jnp.where(upper, first.astype(jnp.float32), second.astype(jnp.float32))
             pairs.append((x.astype(jnp.bfloat16), a, b))
-        scores = []
+        out = []
         for x, a, b in pairs:
             s = dot_t(x, jnp.concatenate([ck[a], ck[b]], axis=0))
-            scores.append(jnp.where(upper, s[:, :BLOCK], s[:, BLOCK:]) * SCALE)
-        highs = [jnp.max(s, axis=1, keepdims=True) for s in scores]
-        weights = [jnp.exp(s - m) for s, m in zip(scores, highs)]
-        totals = [jnp.sum(p, axis=1, keepdims=True) for p in weights]
-        for n, ((x, a, b), p, m, t) in enumerate(zip(pairs, weights, highs, totals)):
+            out.append((jnp.where(upper, s[:, :BLOCK], s[:, BLOCK:]) * SCALE, a, b))
+        return out
+
+    def weights_of(scores):
+        highs = [jnp.max(s, axis=1, keepdims=True) for s, _, _ in scores]
+        return [(jnp.exp(s - m), m, a, b) for (s, a, b), m in zip(scores, highs)]
+
+    def send_back(jz, weights):
+        totals = [jnp.sum(p, axis=1, keepdims=True) for p, _, _, _ in weights]
+        for n, ((p, m, a, b), t) in enumerate(zip(weights, totals)):
             both = high_low(
                 jnp.concatenate([jnp.where(upper, p, 0.0), jnp.where(upper, 0.0, p)], axis=1)
             )
@@ -234,38 +261,25 @@
             two = jnp.sum(jnp.where(m_second, m, jnp.where(t_second, t, 0.0)), axis=0, keepdims=True)
             res_out[jz * 8 + 2 * n] = jnp.where(upper, o, one)
             res_out[jz * 8 + 2 * n + 1] = jnp.where(upper, pltpu.roll(o, PER_KV, 0), two)
-
-    for jz in range(NZ):
-        for i in range(8):
-            if jz + i:
-                message(jz * 8 + i).wait_recv()
-            else:
-                own_message.wait()
-        far(jz)
         for i in range(8):
             if jz + i:
                 result(jz * 8 + i).start()
             else:
                 own_result.start()
 
-    slots = []
-    for r in range(ROWS):
-        for h in range(HEADS):
-            for k in range(TOP):
-                owner = lax.div(sel_ref[r, h, k], 2)
-                oy = lax.div(owner, NZ * NC)
-                oz = lax.rem(lax.div(owner, NC), NZ)
-                dc = lax.rem(owner + c, NC)
-                dy, dz = lax.rem(oy - y + NY, NY), lax.rem(oz - z + NZ, NZ)
-                jy = jnp.where(dy == 0, 0, jnp.where(dy <= NY // 2, 2 * dy - 1, 2 * (NY - dy)))
-                jz = jnp.where(dz == 0, 0, jnp.where(dz <= NZ // 2, 2 * dz - 1, 2 * (NZ - dz)))
-                slots.append((jz * NY + jy) * NC + dc)
+    scores, weights = {}, {}
+    for step in range(NZ + 2):
+        if step < NZ:
+            scores[step] = scores_of(step)
+        if 0 <= step - 1 < NZ:
+            weights[step - 1] = weights_of(scores[step - 1])
+        if 0 <= step - 2:
+            send_back(step - 2, weights[step - 2])
 
     for near in nears:
         near.wait()
-    own_result.wait()
-    for j in order:
-        result(j).wait_recv()
+    returned = pl.ds(0, RES)
+    pltpu.make_async_copy(res_out.at[:, returned], res_in.at[:, returned], res_recv).wait()
 
     for r in range(ROWS):
         for h in range(HEADS):
@@ -298,10 +312,13 @@
         weight = weight + factor * total
     out_ref[...] = (summed / weight).astype(out_ref.dtype)
 
-    for j in order:
-        message(j).wait_send()
-    for j in order:
-        result(j).wait_send()
+    write = pltpu.make_async_copy(out_ref, out_hbm, out_sem)
+    write.start()
+    others = pl.ds(1, PEERS - 1)
+    for buffer, rows, sem in ((msg_out, MSG, msg_send), (res_out, RES, res_send)):
+        sent = buffer.at[others, pl.ds(0, rows)]
+        pltpu.make_async_copy(sent, sent, sem).wait()
+    write.wait()
 
 
 def per_device(queries, request_of, selected, cache_keys, cache_values, recent_keys, recent_values):
@@ -314,10 +331,12 @@
     out = pl.pallas_call(
         kernel,
         out_shape=jax.ShapeDtypeStruct((32, HD), bf16),
-        in_specs=[pl.BlockSpec(memory_space=pltpu.SMEM)] * 2
-        + [pl.BlockSpec(memory_space=pltpu.HBM)] * 5,
-        out_specs=pl.BlockSpec(memory_space=pltpu.VMEM),
+        in_specs=[pl.BlockSpec(memory_space=pltpu.HBM)] * 7,
+        out_specs=pl.BlockSpec(memory_space=pltpu.HBM),
         scratch_shapes=[
+            pltpu.SMEM((ROWS, HEADS, TOP), jnp.int32),
+            pltpu.SMEM((ROWS,), jnp.int32),
+            vmem((32, HD), bf16),
             vmem((128, HD), bf16),
             vmem((PEERS, BLOCK, HD), bf16),
             vmem((PEERS, BLOCK, HD), bf16),
@@ -332,11 +351,12 @@
             vmem((NG, HEADS, 2, 16, HD), f32),
             vmem((TOP, 32, HD), f32),
             vmem((TOP, 32, HD), f32),
-            dma((5,)),
-            dma((PEERS,)),
-            dma((PEERS,)),
-            dma((PEERS,)),
-            dma((PEERS,)),
+            dma((7,)),
+            dma,
+            dma,
+            dma((NZ,)),
+            dma,
+            dma,
             dma((NG,)),
             dma((NG,)),
         ],

time: 32.1 us -> 28.7 us (0.89)
  Pallas kernels: 30.6 us -> 27.2 us
    pallas_call x1, Pallas kernels: 30.6 us -> 27.2 us  [per_device(): pl.pallas_call(kernel, out_shape=jax.ShapeDtypeStruct((32, HD), bf16), in...]
where the time goes in v3:
time: 28.7 us; the launch traced here: 28.5 us
  Pallas kernels  27.2 us (95%)
  local copies, waits for them, and re-layouts  1.3 us (5%)
    pallas_call x1, Pallas kernels, per_device(): pl.pallas_call(kernel, out_shape=jax.ShapeDtypeStruct((32, HD), bf16), in...  27.2 us
    unnamed x1, local copies, waits for them, and re-layouts  1.3 us

profile of v3, /device:TPU:1, one launch (start us, length us, event | category | flops | bytes accessed | tf_op | source)
XLA Modules:
  0.0 28.5 jit_solution(10149369497611087673)
XLA Ops:
  0.0 27.2 %shard_map.73 = bf16[32,128]{1,0:T(8,128)(2,1)} custom-call(s32[4,2,4]{2,1,0:T(2,128)} %sel_hbm.1, s32[4]{0:T(128)} %req_hbm.1, bf16[128,128]{1,0:T(8,128)(2,1)} %bitcast.18, bf16[64,128,128]{2,1,0:T(8,128)(2,1)} %bitcast.14, bf16[64,128,128]{2,1,0:T(8,128)(2,1)} %bitcast.15, bf16[32,256,128]{2,1,0:T(8,128)(2,1)} %bitcast.16, bf16[32,256,128]{2,1,0:T(8,128)(2,1)} %bitcast.17), custom_call_target="tpu_custom_call" | custom-call | tf_op jit(solution)/shard_map/pallas_call | solution.py:331
  27.2 1.3 %copy.11 = bf16[4,1024]{1,0:T(4,128)(2,1)} copy(bf16[4,1024]{1,0:T(4,128)(2,1)} %bitcast.19) | data formatting | bytes 16384

commit v4 on v3

--- a/solution.py
+++ b/solution.py
@@ -16,11 +16,21 @@
 SCALE = HD ** (-0.5)
 MSG = 6
 RES = 5
+AHEAD = 2
 WANTED = ROWS * HEADS * TOP
 
 
 def signed(j):
     return ((j + 1) // 2) * (2 * (j % 2) - 1)
+
+
+def hops(chip):
+    return abs(signed(chip // NY)) + abs(signed(chip % NY))
+
+
+CHIPS = sorted(range(NY * NZ), key=hops)
+WAVES = [[chip for chip in CHIPS if hops(chip) in at] for at in ((0, 1), (2,), (3,), (4,), (5,), (6,))]
+WAVE_OF = {chip: n for n, wave in enumerate(WAVES) for chip in wave}
 
 
 def iota(shape, dim):
@@ -65,7 +75,7 @@
         return (other_z[jz] + other_yc[jy * NC + jc], group)
 
     barrier = pltpu.get_barrier_semaphore()
-    order = range(PEERS - 1, 0, -1)
+    order = [2 * chip + i for chip in reversed(CHIPS) for i in (1, 0) if chip + i]
     for j in order:
         pl.semaphore_signal(barrier, inc=1, device_id=ahead(j), device_id_type=MESH)
     for dg in range(1, NG):
@@ -99,7 +109,7 @@
             for k in range(TOP):
                 e = (r * HEADS + h) * TOP + k
                 block = sel_ref[r, h, k]
-                owner = lax.div(block, 2)
+                owner = lax.shift_right_logical(block, 1)
                 wanted_by[k] = jnp.where(here, owner, wanted_by[k])
                 wanted_by[0] = jnp.where(lane == 32 + e, owner, wanted_by[0])
                 code = prompt * 4 + h * 2 + (block - owner * 2) + 1
@@ -135,7 +145,7 @@
             src_ref=msg_out.at[j, at],
             dst_ref=msg_in.at[j, at],
             send_sem=msg_send,
-            recv_sem=msg_recv.at[j // 8],
+            recv_sem=msg_recv.at[WAVE_OF[j // 2]],
             device_id=ahead(j),
             device_id_type=MESH,
         )
@@ -147,31 +157,20 @@
     )
     own_message.start()
 
-    slots = []
-    for r in range(ROWS):
-        for h in range(HEADS):
-            for k in range(TOP):
-                owner = lax.div(sel_ref[r, h, k], 2)
-                oy = lax.div(owner, NZ * NC)
-                oz = lax.rem(lax.div(owner, NC), NZ)
-                dc = lax.rem(owner + c, NC)
-                dy, dz = lax.rem(oy - y + NY, NY), lax.rem(oz - z + NZ, NZ)
-                jy = jnp.where(dy == 0, 0, jnp.where(dy <= NY // 2, 2 * dy - 1, 2 * (NY - dy)))
-                jz = jnp.where(dz == 0, 0, jnp.where(dz <= NZ // 2, 2 * dz - 1, 2 * (NZ - dz)))
-                slots.append((jz * NY + jy) * NC + dc)
-
     loads[3].wait()
     loads[4].wait()
     row16 = iota((16, RECENT), 0) % ROWS
     row32 = iota((32, HD), 0) % ROWS
     lane16 = iota((16, HD), 1)
 
-    def recent(h, carry):
-        x = q_ref[pl.ds(pl.multiple_of(h * 16, 16), 16), :]
+    def recent_scores(h):
+        x = q_ref[h * 16 : (h + 1) * 16, :]
         s = dot_t(x, rk[h])
         for r in range(1, ROWS):
             s = jnp.where(row16 == r, dot_t(x, rk[r * KVH + h]), s)
-        s = s * SCALE
+        return s * SCALE
+
+    def recent_rest(h, s):
         m = jnp.max(s, axis=1, keepdims=True)
         p = jnp.exp(s - m)
         total = jnp.sum(p, axis=1, keepdims=True)
@@ -181,9 +180,14 @@
             o = jnp.where(row32 == r, dot(both, rv[r * KVH + h]), o)
         near_out[h, 0] = o[0:16] + o[16:32]
         near_out[h, 1] = jnp.where(lane16 < 64, m, total)
-        return carry
-
-    lax.fori_loop(0, KVH, recent, 0)
+
+    pending = []
+    for h in range(KVH):
+        pending.append((h, recent_scores(h)))
+        if h >= AHEAD:
+            recent_rest(*pending.pop(0))
+    for item in pending:
+        recent_rest(*item)
 
     nears = []
     for dg in range(1, NG):
@@ -207,7 +211,7 @@
     def result(j):
         return pltpu.make_async_remote_copy(
             src_ref=res_out.at[j, pl.ds(0, RES)],
-            dst_ref=res_in.at[j, pl.ds(0, RES)],
+            dst_ref=res_in.at[cache, pl.ds(0, RES)],
             send_sem=res_send,
             recv_sem=res_recv,
             device_id=behind(j),
@@ -215,7 +219,7 @@
         )
 
     own_result = pltpu.make_async_copy(
-        res_out.at[0, pl.ds(0, RES)], res_in.at[0, pl.ds(0, RES)], res_recv
+        res_out.at[0, pl.ds(0, RES)], res_in.at[cache, pl.ds(0, RES)], res_recv
     )
     row8 = iota((8, 128), 0)
     upper = row8 < PER_KV
@@ -228,30 +232,24 @@
         code = x[row : row + 1, :].astype(jnp.float32)[0, 0].astype(jnp.int32)
         return jnp.clip(code - 1, 0, PEERS - 1)
 
-    def scores_of(jz):
-        msgs = pl.ds(jz * 8, 8)
-        pltpu.make_async_copy(
-            msg_out.at[msgs, pl.ds(0, MSG)], msg_in.at[msgs, pl.ds(0, MSG)], msg_recv.at[jz]
-        ).wait()
+    def far(n):
+        wave = WAVES[n]
+        arrived = msg_in.at[pl.ds(0, 2 * len(wave)), pl.ds(0, MSG)]
+        pltpu.make_async_copy(arrived, arrived, msg_recv.at[n]).wait()
         pairs = []
-        for i in range(0, 8, 2):
-            first, second = msg_in[jz * 8 + i], msg_in[jz * 8 + i + 1]
+        for chip in wave:
+            first, second = msg_in[2 * chip], msg_in[2 * chip + 1]
             a, b = block_of(first, 4), block_of(second, 3)
             x = jnp.where(upper, first.astype(jnp.float32), second.astype(jnp.float32))
             pairs.append((x.astype(jnp.bfloat16), a, b))
-        out = []
+        scores = []
         for x, a, b in pairs:
             s = dot_t(x, jnp.concatenate([ck[a], ck[b]], axis=0))
-            out.append((jnp.where(upper, s[:, :BLOCK], s[:, BLOCK:]) * SCALE, a, b))
-        return out
-
-    def weights_of(scores):
-        highs = [jnp.max(s, axis=1, keepdims=True) for s, _, _ in scores]
-        return [(jnp.exp(s - m), m, a, b) for (s, a, b), m in zip(scores, highs)]
-
-    def send_back(jz, weights):
-        totals = [jnp.sum(p, axis=1, keepdims=True) for p, _, _, _ in weights]
-        for n, ((p, m, a, b), t) in enumerate(zip(weights, totals)):
+            scores.append(jnp.where(upper, s[:, :BLOCK], s[:, BLOCK:]) * SCALE)
+        highs = [jnp.max(s, axis=1, keepdims=True) for s in scores]
+        weights = [jnp.exp(s - m) for s, m in zip(scores, highs)]
+        totals = [jnp.sum(p, axis=1, keepdims=True) for p in weights]
+        for chip, (x, a, b), p, m, t in zip(wave, pairs, weights, highs, totals):
             both = high_low(
                 jnp.concatenate([jnp.where(upper, p, 0.0), jnp.where(upper, 0.0, p)], axis=1)
             )
@@ -259,22 +257,17 @@
             o = o[0:8] + o[8:16]
             one = jnp.sum(jnp.where(m_first, m, jnp.where(t_first, t, 0.0)), axis=0, keepdims=True)
             two = jnp.sum(jnp.where(m_second, m, jnp.where(t_second, t, 0.0)), axis=0, keepdims=True)
-            res_out[jz * 8 + 2 * n] = jnp.where(upper, o, one)
-            res_out[jz * 8 + 2 * n + 1] = jnp.where(upper, pltpu.roll(o, PER_KV, 0), two)
-        for i in range(8):
-            if jz + i:
-                result(jz * 8 + i).start()
-            else:
-                own_result.start()
-
-    scores, weights = {}, {}
-    for step in range(NZ + 2):
-        if step < NZ:
-            scores[step] = scores_of(step)
-        if 0 <= step - 1 < NZ:
-            weights[step - 1] = weights_of(scores[step - 1])
-        if 0 <= step - 2:
-            send_back(step - 2, weights[step - 2])
+            res_out[2 * chip] = jnp.where(upper, o, one)
+            res_out[2 * chip + 1] = jnp.where(upper, pltpu.roll(o, PER_KV, 0), two)
+        for chip in reversed(wave):
+            for i in (1, 0):
+                if chip + i:
+                    result(2 * chip + i).start()
+                else:
+                    own_result.start()
+
+    for n in range(len(WAVES)):
+        far(n)
 
     for near in nears:
         near.wait()
@@ -284,8 +277,7 @@
     for r in range(ROWS):
         for h in range(HEADS):
             for k in range(TOP):
-                e = (r * HEADS + h) * TOP + k
-                tile = res_in[slots[e]]
+                tile = res_in[lax.shift_right_logical(sel_ref[r, h, k], 1)]
                 rows = pl.ds(h * 16 + r, 4, stride=4)
                 far_o[k, rows, :] = tile[0:4]
                 far_s[k, rows, :] = jnp.broadcast_to(tile[4:5], (4, 128))
@@ -354,7 +346,7 @@
             dma((7,)),
             dma,
             dma,
-            dma((NZ,)),
+            dma((len(WAVES),)),
             dma,
             dma,
             dma((NG,)),

time: 28.7 us -> 27.2 us (0.948)
  Pallas kernels: 27.2 us -> 25.7 us
    pallas_call x1, Pallas kernels: 27.2 us -> 25.7 us  [per_device(): pl.pallas_call(kernel, out_shape=jax.ShapeDtypeStruct((32, HD), bf16), in...]
where the time goes in v4:
time: 27.2 us; the launch traced here: 27.1 us
  Pallas kernels  25.7 us (94%)
  local copies, waits for them, and re-layouts  1.3 us (5%)
    pallas_call x1, Pallas kernels, per_device(): pl.pallas_call(kernel, out_shape=jax.ShapeDtypeStruct((32, HD), bf16), in...  25.7 us
    unnamed x1, local copies, waits for them, and re-layouts  1.3 us

profile of v4, /device:TPU:1, one launch (start us, length us, event | category | flops | bytes accessed | tf_op | source)
XLA Modules:
  0.0 27.1 jit_solution(1803053973530322152)
XLA Ops:
  0.0 25.7 %shard_map.73 = bf16[32,128]{1,0:T(8,128)(2,1)} custom-call(s32[4,2,4]{2,1,0:T(2,128)} %sel_hbm.1, s32[4]{0:T(128)} %req_hbm.1, bf16[128,128]{1,0:T(8,128)(2,1)} %bitcast.18, bf16[64,128,128]{2,1,0:T(8,128)(2,1)} %bitcast.14, bf16[64,128,128]{2,1,0:T(8,128)(2,1)} %bitcast.15, bf16[32,256,128]{2,1,0:T(8,128)(2,1)} %bitcast.16, bf16[32,256,128]{2,1,0:T(8,128)(2,1)} %bitcast.17), custom_call_target="tpu_custom_call" | custom-call | tf_op jit(solution)/shard_map/pallas_call | solution.py:323
  25.8 1.3 %copy.11 = bf16[4,1024]{1,0:T(4,128)(2,1)} copy(bf16[4,1024]{1,0:T(4,128)(2,1)} %bitcast.19) | data formatting | bytes 16384

commit v5 on v4

--- a/solution.py
+++ b/solution.py
@@ -52,9 +52,9 @@
 
 
 def kernel(
-    sel_hbm, req_hbm, q_hbm, ck_ref, cv_ref, rk_ref, rv_ref, out_hbm,
-    sel_ref, req_ref, out_ref, q_ref, ck, cv, rk, rv, rhs, msg_out, msg_in, res_out, res_in, near_out, near_in, far_o, far_s,
-    load_sem, out_sem, msg_send, msg_recv, res_send, res_recv, near_send, near_recv,
+    sel_hbm, req_hbm, q_hbm, ck_ref, cv_ref, rk_ref, rv_ref, out_ref,
+    sel_ref, req_ref, q_ref, ck, cv, rk, rv, rhs, msg_out, msg_in, res_out, res_in, near_out, near_in, far_o, far_s,
+    load_sem, msg_send, msg_recv, res_send, res_recv, near_send, near_recv,
 ):
     cache = lax.axis_index("cache")
     group = lax.axis_index("group")
@@ -271,6 +271,26 @@
 
     for near in nears:
         near.wait()
+
+    def merged(parts):
+        peak = functools.reduce(jnp.maximum, [m for _, m, _ in parts])
+        summed, weight = 0.0, 0.0
+        for o, m, total in parts:
+            factor = jnp.exp(m - peak)
+            summed = summed + factor * o
+            weight = weight + factor * total
+        return summed, peak, weight
+
+    parts = []
+    for dg in range(NG):
+        if dg:
+            both = near_in[dg]
+        else:
+            both = near_out[pl.ds(group * HEADS, HEADS)]
+        stat = both[:, 1].reshape(32, 128)
+        parts.append((both[:, 0].reshape(32, 128), stat[:, 0:1], stat[:, 64:65]))
+    parts = [merged(parts)]
+
     returned = pl.ds(0, RES)
     pltpu.make_async_copy(res_out.at[:, returned], res_in.at[:, returned], res_recv).wait()
 
@@ -283,34 +303,18 @@
                 far_s[k, rows, :] = jnp.broadcast_to(tile[4:5], (4, 128))
     lane32 = iota((32, 128), 1)
     which = iota((32, 128), 0) // 4 % 4
-    parts = []
     for k in range(TOP):
         stat = far_s[k]
         m = jnp.sum(jnp.where(lane32 == which, stat, 0.0), axis=1, keepdims=True)
         total = jnp.sum(jnp.where(lane32 == which + PER_KV, stat, 0.0), axis=1, keepdims=True)
         parts.append((far_o[k], m, total))
-    for dg in range(NG):
-        if dg:
-            both = near_in[dg]
-        else:
-            both = near_out[pl.ds(group * HEADS, HEADS)]
-        stat = both[:, 1].reshape(32, 128)
-        parts.append((both[:, 0].reshape(32, 128), stat[:, 0:1], stat[:, 64:65]))
-    peak = functools.reduce(jnp.maximum, [m for _, m, _ in parts])
-    summed, weight = 0.0, 0.0
-    for o, m, total in parts:
-        factor = jnp.exp(m - peak)
-        summed = summed + factor * o
-        weight = weight + factor * total
+    summed, _, weight = merged(parts)
     out_ref[...] = (summed / weight).astype(out_ref.dtype)
 
-    write = pltpu.make_async_copy(out_ref, out_hbm, out_sem)
-    write.start()
     others = pl.ds(1, PEERS - 1)
     for buffer, rows, sem in ((msg_out, MSG, msg_send), (res_out, RES, res_send)):
         sent = buffer.at[others, pl.ds(0, rows)]
         pltpu.make_async_copy(sent, sent, sem).wait()
-    write.wait()
 
 
 def per_device(queries, request_of, selected, cache_keys, cache_values, recent_keys, recent_values):
@@ -324,11 +328,10 @@
         kernel,
         out_shape=jax.ShapeDtypeStruct((32, HD), bf16),
         in_specs=[pl.BlockSpec(memory_space=pltpu.HBM)] * 7,
-        out_specs=pl.BlockSpec(memory_space=pltpu.HBM),
+        out_specs=pl.BlockSpec(memory_space=pltpu.VMEM),
         scratch_shapes=[
             pltpu.SMEM((ROWS, HEADS, TOP), jnp.int32),
             pltpu.SMEM((ROWS,), jnp.int32),
-            vmem((32, HD), bf16),
             vmem((128, HD), bf16),
             vmem((PEERS, BLOCK, HD), bf16),
             vmem((PEERS, BLOCK, HD), bf16),
@@ -345,7 +348,6 @@
             vmem((TOP, 32, HD), f32),
             dma((7,)),
             dma,
-            dma,
             dma((len(WAVES),)),
             dma,
             dma,
@@ -353,11 +355,16 @@
             dma((NG,)),
         ],
         compiler_params=pltpu.CompilerParams(
-            collective_id=0, has_side_effects=True, vmem_limit_bytes=67043328
+            collective_id=0, has_side_effects=True, vmem_limit_bytes=40 * 1024 * 1024
         ),
     )(
-        selected, request_of, q, blocks(cache_keys), blocks(cache_values),
-        recents(recent_keys), recents(recent_values),
+        *[
+            pltpu.with_memory_space_constraint(a, pltpu.HBM)
+            for a in (
+                selected, request_of, q, blocks(cache_keys), blocks(cache_values),
+                recents(recent_keys), recents(recent_values),
+            )
+        ]
     )
     return out.reshape(HEADS * PER_KV, ROWS, HD).transpose(1, 0, 2).reshape(ROWS, HEADS * PER_KV * HD)
 

time: 27.2 us -> 25.8 us (0.949)
  local copies, waits for them, and re-layouts: 1.3 us -> 0.6 us
  Pallas kernels: 25.7 us -> 25.1 us
    unnamed x1, local copies, waits for them, and re-layouts: 1.3 us -> 0.6 us
    pallas_call x1, Pallas kernels: 25.7 us -> 25.1 us  [per_device(): pl.pallas_call(kernel, out_shape=jax.ShapeDtypeStruct((32, HD), bf16), in...]
where the time goes in v5:
time: 25.8 us; the launch traced here: 25.7 us
  Pallas kernels  25.1 us (97%)
  local copies, waits for them, and re-layouts  0.6 us (2%)
    pallas_call x1, Pallas kernels, per_device(): pl.pallas_call(kernel, out_shape=jax.ShapeDtypeStruct((32, HD), bf16), in...  25.1 us
    unnamed x1, local copies, waits for them, and re-layouts  0.6 us

profile of v5, /device:TPU:1, one launch (start us, length us, event | category | flops | bytes accessed | tf_op | source)
XLA Modules:
  0.0 25.7 jit_solution(13857495581141625737)
XLA Ops:
  0.0 25.1 %shard_map.73 = bf16[32,128]{1,0:T(8,128)(2,1)S(1)} custom-call(s32[4,2,4]{2,1,0:T(2,128)} %sel_hbm.1, s32[4]{0:T(128)} %req_hbm.1, bf16[128,128]{1,0:T(8,128)(2,1)} %bitcast.19, bf16[64,128,128]{2,1,0:T(8,128)(2,1)} %bitcast.15, bf16[64,128,128]{2,1,0:T(8,128)(2,1)} %bitcast.16, bf16[32,256,128]{2,1,0:T(8,128)(2,1)} %bitcast.17, bf16[32,256,128]{2,1,0:T(8,128)(2,1)} %bitcast.18), custom_call_target="tpu_custom_call" | custom-call | tf_op jit(solution)/shard_map/pallas_call | solution.py:327
  25.1 0.6 %copy.11 = bf16[4,1024]{1,0:T(4,128)(2,1)} copy(bf16[4,1024]{1,0:T(4,128)(2,1)S(1)} %bitcast.14) | data formatting | bytes 16384

commit v6 on v5

--- a/solution.py
+++ b/solution.py
@@ -17,6 +17,7 @@
 MSG = 6
 RES = 5
 AHEAD = 2
+URGENT = 4
 WANTED = ROWS * HEADS * TOP
 
 
@@ -232,6 +233,17 @@
         code = x[row : row + 1, :].astype(jnp.float32)[0, 0].astype(jnp.int32)
         return jnp.clip(code - 1, 0, PEERS - 1)
 
+    def urgent(jz):
+        return other_z[opposite(jz, NZ)] < URGENT * NC
+
+    def send_back(chips):
+        for chip in reversed(chips):
+            for i in (1, 0):
+                if chip + i:
+                    result(2 * chip + i).start()
+                else:
+                    own_result.start()
+
     def far(n):
         wave = WAVES[n]
         arrived = msg_in.at[pl.ds(0, 2 * len(wave)), pl.ds(0, MSG)]
@@ -259,15 +271,16 @@
             two = jnp.sum(jnp.where(m_second, m, jnp.where(t_second, t, 0.0)), axis=0, keepdims=True)
             res_out[2 * chip] = jnp.where(upper, o, one)
             res_out[2 * chip + 1] = jnp.where(upper, pltpu.roll(o, PER_KV, 0), two)
-        for chip in reversed(wave):
-            for i in (1, 0):
-                if chip + i:
-                    result(2 * chip + i).start()
-                else:
-                    own_result.start()
+        for jz in range(NZ):
+            chips = [chip for chip in wave if chip // NY == jz]
+            if chips:
+                pl.when(urgent(jz))(lambda: send_back(chips))
 
     for n in range(len(WAVES)):
         far(n)
+    for jz in reversed(range(NZ)):
+        chips = [chip for chip in CHIPS if chip // NY == jz]
+        pl.when(jnp.logical_not(urgent(jz)))(lambda: send_back(chips))
 
     for near in nears:
         near.wait()

time: 25.8 us -> 25.4 us (0.984)
  Pallas kernels: 25.1 us -> 24.7 us
    pallas_call x1, Pallas kernels: 25.1 us -> 24.7 us  [per_device(): pl.pallas_call(kernel, out_shape=jax.ShapeDtypeStruct((32, HD), bf16), in...]
where the time goes in v6:
time: 25.4 us
  Pallas kernels  24.7 us (97%)
  local copies, waits for them, and re-layouts  0.6 us (2%)
    pallas_call x1, Pallas kernels, per_device(): pl.pallas_call(kernel, out_shape=jax.ShapeDtypeStruct((32, HD), bf16), in...  24.7 us
    unnamed x1, local copies, waits for them, and re-layouts  0.6 us

profile of v6, /device:TPU:1, one launch (start us, length us, event | category | flops | bytes accessed | tf_op | source)
XLA Modules:
  0.0 25.4 jit_solution(6325577086527480083)
XLA Ops:
  0.0 24.7 %shard_map.73 = bf16[32,128]{1,0:T(8,128)(2,1)S(1)} custom-call(s32[4,2,4]{2,1,0:T(2,128)} %sel_hbm.1, s32[4]{0:T(128)} %req_hbm.1, bf16[128,128]{1,0:T(8,128)(2,1)} %bitcast.19, bf16[64,128,128]{2,1,0:T(8,128)(2,1)} %bitcast.15, bf16[64,128,128]{2,1,0:T(8,128)(2,1)} %bitcast.16, bf16[32,256,128]{2,1,0:T(8,128)(2,1)} %bitcast.17, bf16[32,256,128]{2,1,0:T(8,128)(2,1)} %bitcast.18), custom_call_target="tpu_custom_call" | custom-call | tf_op jit(solution)/shard_map/pallas_call | solution.py:340
  24.8 0.6 %copy.11 = bf16[4,1024]{1,0:T(4,128)(2,1)} copy(bf16[4,1024]{1,0:T(4,128)(2,1)S(1)} %bitcast.14) | data formatting | bytes 16384

commit v7 on v6

--- a/solution.py
+++ b/solution.py
@@ -138,6 +138,38 @@
         pick = jnp.where(hit & row_match, 1.0, 0.0).astype(jnp.bfloat16)
         msg_out[jz * 8 : (jz + 1) * 8] = dot(pick, table).reshape(8, 8, 128).astype(jnp.bfloat16)
 
+    loads[3].wait()
+    loads[4].wait()
+    row16 = iota((16, RECENT), 0) % ROWS
+    row32 = iota((32, HD), 0) % ROWS
+    lane16 = iota((16, HD), 1)
+
+    def recent_scores(h):
+        x = q_ref[h * 16 : (h + 1) * 16, :]
+        s = dot_t(x, rk[h])
+        for r in range(1, ROWS):
+            s = jnp.where(row16 == r, dot_t(x, rk[r * KVH + h]), s)
+        return s * SCALE
+
+    def recent_rest(h, s):
+        m = jnp.max(s, axis=1, keepdims=True)
+        p = jnp.exp(s - m)
+        total = jnp.sum(p, axis=1, keepdims=True)
+        both = high_low(p)
+        o = dot(both, rv[h])
+        for r in range(1, ROWS):
+            o = jnp.where(row32 == r, dot(both, rv[r * KVH + h]), o)
+        near_out[h, 0] = o[0:16] + o[16:32]
+        near_out[h, 1] = jnp.where(lane16 < 64, m, total)
+
+    pending = []
+    for h in range(KVH):
+        pending.append((h, recent_scores(h)))
+        if h >= AHEAD:
+            recent_rest(*pending.pop(0))
+    for item in pending:
+        recent_rest(*item)
+
     pl.semaphore_wait(barrier, PEERS - 1 + NG - 1)
 
     def message(j):
@@ -151,44 +183,12 @@
             device_id_type=MESH,
         )
 
-    for j in order:
+    for j in order[:10] + order[:9:-1]:
         message(j).start()
     own_message = pltpu.make_async_copy(
         msg_out.at[0, pl.ds(0, MSG)], msg_in.at[0, pl.ds(0, MSG)], msg_recv.at[0]
     )
     own_message.start()
-
-    loads[3].wait()
-    loads[4].wait()
-    row16 = iota((16, RECENT), 0) % ROWS
-    row32 = iota((32, HD), 0) % ROWS
-    lane16 = iota((16, HD), 1)
-
-    def recent_scores(h):
-        x = q_ref[h * 16 : (h + 1) * 16, :]
-        s = dot_t(x, rk[h])
-        for r in range(1, ROWS):
-            s = jnp.where(row16 == r, dot_t(x, rk[r * KVH + h]), s)
-        return s * SCALE
-
-    def recent_rest(h, s):
-        m = jnp.max(s, axis=1, keepdims=True)
-        p = jnp.exp(s - m)
-        total = jnp.sum(p, axis=1, keepdims=True)
-        both = high_low(p)
-        o = dot(both, rv[h])
-        for r in range(1, ROWS):
-            o = jnp.where(row32 == r, dot(both, rv[r * KVH + h]), o)
-        near_out[h, 0] = o[0:16] + o[16:32]
-        near_out[h, 1] = jnp.where(lane16 < 64, m, total)
-
-    pending = []
-    for h in range(KVH):
-        pending.append((h, recent_scores(h)))
-        if h >= AHEAD:
-            recent_rest(*pending.pop(0))
-    for item in pending:
-        recent_rest(*item)
 
     nears = []
     for dg in range(1, NG):

time: 25.4 us -> 24.8 us (0.976)
  Pallas kernels: 24.7 us -> 24.1 us
    pallas_call x1, Pallas kernels: 24.7 us -> 24.1 us  [per_device(): pl.pallas_call(kernel, out_shape=jax.ShapeDtypeStruct((32, HD), bf16), in...]
where the time goes in v7:
time: 24.8 us; the launch traced here: 24.7 us
  Pallas kernels  24.1 us (97%)
  local copies, waits for them, and re-layouts  0.6 us (2%)
    pallas_call x1, Pallas kernels, per_device(): pl.pallas_call(kernel, out_shape=jax.ShapeDtypeStruct((32, HD), bf16), in...  24.1 us
    unnamed x1, local copies, waits for them, and re-layouts  0.6 us

profile of v7, /device:TPU:1, one launch (start us, length us, event | category | flops | bytes accessed | tf_op | source)
XLA Modules:
  0.0 24.7 jit_solution(13729934575353520028)
XLA Ops:
  0.0 24.1 %shard_map.73 = bf16[32,128]{1,0:T(8,128)(2,1)S(1)} custom-call(s32[4,2,4]{2,1,0:T(2,128)} %sel_hbm.1, s32[4]{0:T(128)} %req_hbm.1, bf16[128,128]{1,0:T(8,128)(2,1)} %bitcast.19, bf16[64,128,128]{2,1,0:T(8,128)(2,1)} %bitcast.15, bf16[64,128,128]{2,1,0:T(8,128)(2,1)} %bitcast.16, bf16[32,256,128]{2,1,0:T(8,128)(2,1)} %bitcast.17, bf16[32,256,128]{2,1,0:T(8,128)(2,1)} %bitcast.18), custom_call_target="tpu_custom_call" | custom-call | tf_op jit(solution)/shard_map/pallas_call | solution.py:340
  24.1 0.6 %copy.11 = bf16[4,1024]{1,0:T(4,128)(2,1)} copy(bf16[4,1024]{1,0:T(4,128)(2,1)S(1)} %bitcast.14) | data formatting | bytes 16384

commit v8 on v7

--- a/solution.py
+++ b/solution.py
@@ -30,7 +30,7 @@
 
 
 CHIPS = sorted(range(NY * NZ), key=hops)
-WAVES = [[chip for chip in CHIPS if hops(chip) in at] for at in ((0, 1), (2,), (3,), (4,), (5,), (6,))]
+WAVES = [[chip for chip in CHIPS if hops(chip) in at] for at in ((0, 1, 2), (3,), (4,), (5,), (6,))]
 WAVE_OF = {chip: n for n, wave in enumerate(WAVES) for chip in wave}
 
 

time: 24.8 us -> 24.8 us (level)
  no operation moved by 1% of the time
where the time goes in v8:
time: 24.8 us; the launch traced here: 24.7 us
  Pallas kernels  24.1 us (97%)
  local copies, waits for them, and re-layouts  0.6 us (2%)
    pallas_call x1, Pallas kernels, per_device(): pl.pallas_call(kernel, out_shape=jax.ShapeDtypeStruct((32, HD), bf16), in...  24.1 us
    unnamed x1, local copies, waits for them, and re-layouts  0.6 us

profile of v8, /device:TPU:1, one launch (start us, length us, event | category | flops | bytes accessed | tf_op | source)
XLA Modules:
  0.0 24.7 jit_solution(11198759593786306117)
XLA Ops:
  0.0 24.1 %shard_map.73 = bf16[32,128]{1,0:T(8,128)(2,1)S(1)} custom-call(s32[4,2,4]{2,1,0:T(2,128)} %sel_hbm.1, s32[4]{0:T(128)} %req_hbm.1, bf16[128,128]{1,0:T(8,128)(2,1)} %bitcast.19, bf16[64,128,128]{2,1,0:T(8,128)(2,1)} %bitcast.15, bf16[64,128,128]{2,1,0:T(8,128)(2,1)} %bitcast.16, bf16[32,256,128]{2,1,0:T(8,128)(2,1)} %bitcast.17, bf16[32,256,128]{2,1,0:T(8,128)(2,1)} %bitcast.18), custom_call_target="tpu_custom_call" | custom-call | tf_op jit(solution)/shard_map/pallas_call | solution.py:340
  24.1 0.6 %copy.11 = bf16[4,1024]{1,0:T(4,128)(2,1)} copy(bf16[4,1024]{1,0:T(4,128)(2,1)S(1)} %bitcast.14) | data formatting | bytes 16384
